TPU v7x, 256 devices: a whole 4x4x8 slice. The times are simulated.
256 devices in a mesh: blk: 16 (over z_lo, x), tm: 16 (over y, z_hi, core).
Axes of the slice: x: 4, y: 4, z: 8 (z_hi: 2, z_lo: 4; z = z_hi * 4 + z_lo), core: 2. Of those that a mesh axis runs over, the one named last changes fastest.
Arguments:
- intensity: bfloat16 [3072, 32768], P('tm', 'blk'), may hold values from 0.04 to 330, as said below
- block_cycle: int32 [256], P('blk'), may hold values from 0 to 15, as said below
- cycle_order: int32 [16], replicated, may hold values from 0 to 15, as said below
Outputs:
- twotime: float32 [16, 3072, 3072], P('blk', 'tm')
Inputs may be any that keep to these rules, and one draw needn't show every extreme that they name: `intensity`: positive corrected intensities. `block_cycle`: every cycle holds 1 to 31 blocks of the whole detector, and some cycle exactly 31; the 16 blocks of one index of blk hold at most 2 blocks of one cycle, and exactly 2 for some cycle. `cycle_order`: each cycle once.
All inputs are finite; a program needn't handle non-finite values.
Results may differ from a plain program's by a relative error of at most 0.0003.
Values may be sent and summed in bfloat16 or wider, within the bound.
A program may use at most 64 MiB of HBM per device.

v0:
```python
import jax
import jax.numpy as jnp
from jax import lax
from jax.sharding import PartitionSpec as P

BLOCK = 128
RCAP = 31


def from_behind(x, axis, by):
    count = lax.axis_size(axis)
    return lax.ppermute(x, axis, [(i, (i + by) % count) for i in range(count)])


def gram(left, right):
    return lax.dot_general(
        left, right, (((1,), (1,)), ((), ())), preferred_element_type=jnp.float32
    )


def on_device(intensity, block_cycle, cycle_order):
    panel = intensity.shape[0]
    blk_dev = block_cycle.shape[0]
    cycles = cycle_order.shape[0]
    groups = lax.axis_size("blk")
    steps = lax.axis_size("tm")
    me_tm = lax.axis_index("tm")
    frames = panel * steps
    most_here = 2 * max(1, blk_dev // cycles)
    local = intensity.reshape(panel, blk_dev, BLOCK)
    cycle_ids = jnp.arange(cycles, dtype=jnp.int32)
    position = jnp.sum(
        jnp.where(cycle_order[None, :] == block_cycle[:, None], cycle_ids[None, :], 0), axis=1
    )
    block_ids = jnp.arange(blk_dev, dtype=jnp.int32)
    same = block_cycle[:, None] == block_cycle[None, :]
    earlier = block_ids[None, :] < block_ids[:, None]
    rank = jnp.sum(jnp.logical_and(same, earlier).astype(jnp.int32), axis=1)
    slot = position * most_here + rank
    slot_ids = jnp.arange(cycles * most_here, dtype=jnp.int32)
    hits = slot[None, :] == slot_ids[:, None]
    source = jnp.sum(jnp.where(hits, block_ids[None, :], 0), axis=1)
    filled = jnp.any(hits, axis=1)
    outgoing = jnp.where(
        filled[None, :, None], jnp.take(local, source, axis=1), jnp.zeros((), jnp.bfloat16)
    )
    flags = filled.astype(jnp.bfloat16).reshape(1, cycles * most_here, 1)
    arrived, marks = (
        lax.all_to_all(outgoing, "blk", split_axis=1, concat_axis=1, tiled=True),
        lax.all_to_all(flags, "blk", split_axis=1, concat_axis=1, tiled=True),
    )
    slots = groups * most_here
    present = marks.reshape(slots) > 0.5
    idx = jnp.arange(slots, dtype=jnp.int32)
    place = jnp.sum(
        jnp.logical_and(present[None, :], idx[None, :] < idx[:, None]).astype(jnp.int32), axis=1
    )
    compact_ids = jnp.arange(RCAP, dtype=jnp.int32)
    chosen = jnp.logical_and(present[None, :], place[None, :] == compact_ids[:, None])
    pick = jnp.sum(jnp.where(chosen, idx[None, :], 0), axis=1)
    used = jnp.any(chosen, axis=1)
    cycle_rows = jnp.where(
        used[None, :, None], jnp.take(arrived, pick, axis=1), jnp.zeros((), jnp.bfloat16)
    )
    cycle_rows = cycle_rows.reshape(panel, RCAP * BLOCK)
    count = jnp.sum(present.astype(jnp.float32)) * BLOCK
    own_sums = jnp.sum(cycle_rows, axis=1, dtype=jnp.float32)
    all_sums = lax.all_gather(own_sums, "tm", axis=0, tiled=True)
    first = gram(cycle_rows, cycle_rows)
    blank = jnp.zeros((panel, panel), jnp.float32)
    start = lax.dynamic_update_slice(
        jnp.zeros((panel, frames), jnp.float32), first, (0, me_tm * panel)
    )

    def visit(k, carry):
        total, moving = carry
        moving = from_behind(moving, "tm", 1)
        keep = k > me_tm
        column = (me_tm - k + steps) % steps
        tile = lax.cond(keep, lambda: gram(cycle_rows, moving), lambda: blank)
        offset = column * panel
        held = lax.dynamic_slice(total, (0, offset), (panel, panel))
        total = lax.dynamic_update_slice(total, jnp.where(keep, tile, held), (0, offset))
        return (total, moving)

    total, _ = lax.fori_loop(1, steps, visit, (start, cycle_rows))
    column_panel = jnp.arange(frames, dtype=jnp.int32) // panel
    upper_mask = column_panel >= me_tm
    scaled = total * count / (own_sums[:, None] * all_sums[None, :])
    twotime = jnp.where(upper_mask[None, :], scaled, jnp.float32(0.0))
    return twotime.reshape(1, panel, frames)


def solution(mesh):
    placed = (P("tm", "blk"), P("blk"), P())
    return jax.shard_map(
        on_device, mesh=mesh, in_specs=placed, out_specs=P("blk", "tm", None), check_vma=False
    )
```

profile of v0, /device:TPU:4, one launch (start us, length us, event | category | flops | bytes accessed | tf_op | source)
XLA Modules:
  0.0 821.3 jit_solution(3460006705226937804)
XLA Ops:
  1.8 8.9 %all-to-all-start = ((bf16[1,32,1]{2,0,1:T(2,128)(2,1)}), bf16[1,32,1]{2,0,1:T(2,128)(2,1)S(1)}, u32[]{:S(2)}, u32[]{:S(2)}) async-start(bf16[1,32,1]{2,0,1:T(2,128)(2,1)} %copy.14), calls=%async_computation | async-start | bytes 32768 | tf_op jit(solution)/shard_map/all_to_all | solution.py:50
  13.3 3.1 all-to-all-done
  16.3 6.5 all-to-all-start.1
  26.4 29.4 %all-to-all-done.1 = bf16[192,32,128]{2,0,1:T(8,128)(2,1)} async-done(((bf16[192,32,128]{2,0,1:T(8,128)(2,1)}), bf16[192,32,128]{2,0,1:T(8,128)(2,1)}, u32[]{:S(2)}, u32[]{:S(2)}) %all-to-all-start.1) | async-done | bytes 1572896 | tf_op jit(solution)/shard_map/all_to_all | solution.py:49
  55.8 2.2 gather_fusion.1
  61.8 88.5 %all-reduce = f32[3072]{0:T(1024)S(1)} all-reduce(f32[3072]{0:T(1024)S(1)} %dynamic-update-slice), channel_id=1, replica_groups=mesh['blk'=16,'tm'=16] {'tm'}, use_global_device_ids=true, to_apply=%add | all-reduce | flops 3072 | bytes 24576
  153.7 664.1 %while.17 = (s32[]{:T(128)}, f32[192,3072]{1,0:T(8,128)}, bf16[192,3968]{1,0:T(8,128)(2,1)}, s32[]{:T(128)}, bf16[192,3968]{1,0:T(8,128)(2,1)}, /*index=5*/s32[]...) while((s32[]{:T(128)}, f32[192,3072]{1,0:T(8,128)}, ...), condition=%wide.region_10.11_spmd, body=%wide.region_7.10_spmd.sunk | while | flops 292589568 | bytes 13074807 | solution.py:86
  153.7 41.9 %collective-permute-done = bf16[192,3968]{1,0:T(8,128)(2,1)S(1)} collective-permute-done((bf16[192,3968]{1,0:T(8,128)(2,1)}, bf16[192,3968]{1,0:T(8,128)(2,1)S(1)}, u32[]{:S(2)}, u32[]{:S(2)}) %collective-permute-start) | collective-permute-done | bytes 1523744 | tf_op jit(solution)/shard_map/while/body/eval_jaxpr/ppermute | solution.py:12
  195.6 2.0 conditional.2
  195.6 2.0 fusion.14
  198.7 1.8 dynamic_update_slice.15
  201.6 42.3 %collective-permute-done = bf16[192,3968]{1,0:T(8,128)(2,1)S(1)} collective-permute-done((bf16[192,3968]{1,0:T(8,128)(2,1)}, bf16[192,3968]{1,0:T(8,128)(2,1)S(1)}, u32[]{:S(2)}, u32[]{:S(2)}) %collective-permute-start) | collective-permute-done | bytes 1523744 | tf_op jit(solution)/shard_map/while/body/eval_jaxpr/ppermute | solution.py:12
  243.9 2.0 conditional.2
  243.9 2.0 fusion.14
  249.8 47.1 %collective-permute-done = bf16[192,3968]{1,0:T(8,128)(2,1)S(1)} collective-permute-done((bf16[192,3968]{1,0:T(8,128)(2,1)}, bf16[192,3968]{1,0:T(8,128)(2,1)S(1)}, u32[]{:S(2)}, u32[]{:S(2)}) %collective-permute-start) | collective-permute-done | bytes 1523744 | tf_op jit(solution)/shard_map/while/body/eval_jaxpr/ppermute | solution.py:12
  296.9 2.0 conditional.2
  296.9 2.0 fusion.14
  300.0 2.0 dynamic_update_slice.15
  303.1 43.3 %collective-permute-done = bf16[192,3968]{1,0:T(8,128)(2,1)S(1)} collective-permute-done((bf16[192,3968]{1,0:T(8,128)(2,1)}, bf16[192,3968]{1,0:T(8,128)(2,1)S(1)}, u32[]{:S(2)}, u32[]{:S(2)}) %collective-permute-start) | collective-permute-done | bytes 1523744 | tf_op jit(solution)/shard_map/while/body/eval_jaxpr/ppermute | solution.py:12
  346.4 2.0 conditional.2
  346.4 2.0 fusion.14
  349.4 1.8 dynamic_update_slice.15
  352.3 45.7 %collective-permute-done = bf16[192,3968]{1,0:T(8,128)(2,1)S(1)} collective-permute-done((bf16[192,3968]{1,0:T(8,128)(2,1)}, bf16[192,3968]{1,0:T(8,128)(2,1)S(1)}, u32[]{:S(2)}, u32[]{:S(2)}) %collective-permute-start) | collective-permute-done | bytes 1523744 | tf_op jit(solution)/shard_map/while/body/eval_jaxpr/ppermute | solution.py:12
  398.1 2.0 conditional.2
  398.1 2.0 fusion.14
  401.1 2.0 dynamic_update_slice.15
  404.2 43.3 %collective-permute-done = bf16[192,3968]{1,0:T(8,128)(2,1)S(1)} collective-permute-done((bf16[192,3968]{1,0:T(8,128)(2,1)}, bf16[192,3968]{1,0:T(8,128)(2,1)S(1)}, u32[]{:S(2)}, u32[]{:S(2)}) %collective-permute-start) | collective-permute-done | bytes 1523744 | tf_op jit(solution)/shard_map/while/body/eval_jaxpr/ppermute | solution.py:12
  447.5 2.0 conditional.2
  447.5 2.0 fusion.14
  450.6 1.8 dynamic_update_slice.15
  453.5 45.7 %collective-permute-done = bf16[192,3968]{1,0:T(8,128)(2,1)S(1)} collective-permute-done((bf16[192,3968]{1,0:T(8,128)(2,1)}, bf16[192,3968]{1,0:T(8,128)(2,1)S(1)}, u32[]{:S(2)}, u32[]{:S(2)}) %collective-permute-start) | collective-permute-done | bytes 1523744 | tf_op jit(solution)/shard_map/while/body/eval_jaxpr/ppermute | solution.py:12
  499.2 2.0 conditional.2
  499.2 2.0 fusion.14
  502.3 2.0 dynamic_update_slice.15
  505.4 43.3 %collective-permute-done = bf16[192,3968]{1,0:T(8,128)(2,1)S(1)} collective-permute-done((bf16[192,3968]{1,0:T(8,128)(2,1)}, bf16[192,3968]{1,0:T(8,128)(2,1)S(1)}, u32[]{:S(2)}, u32[]{:S(2)}) %collective-permute-start) | collective-permute-done | bytes 1523744 | tf_op jit(solution)/shard_map/while/body/eval_jaxpr/ppermute | solution.py:12
  548.7 2.0 conditional.2
  548.7 2.0 fusion.14
  554.6 45.7 %collective-permute-done = bf16[192,3968]{1,0:T(8,128)(2,1)S(1)} collective-permute-done((bf16[192,3968]{1,0:T(8,128)(2,1)}, bf16[192,3968]{1,0:T(8,128)(2,1)S(1)}, u32[]{:S(2)}, u32[]{:S(2)}) %collective-permute-start) | collective-permute-done | bytes 1523744 | tf_op jit(solution)/shard_map/while/body/eval_jaxpr/ppermute | solution.py:12
  600.4 2.0 conditional.2
  600.4 2.0 fusion.14
  603.5 2.0 dynamic_update_slice.15
  606.6 43.3 %collective-permute-done = bf16[192,3968]{1,0:T(8,128)(2,1)S(1)} collective-permute-done((bf16[192,3968]{1,0:T(8,128)(2,1)}, bf16[192,3968]{1,0:T(8,128)(2,1)S(1)}, u32[]{:S(2)}, u32[]{:S(2)}) %collective-permute-start) | collective-permute-done | bytes 1523744 | tf_op jit(solution)/shard_map/while/body/eval_jaxpr/ppermute | solution.py:12
  649.9 2.0 conditional.2
  649.9 2.0 fusion.14
  652.9 1.8 dynamic_update_slice.15
  655.8 29.4 %collective-permute-done = bf16[192,3968]{1,0:T(8,128)(2,1)S(1)} collective-permute-done((bf16[192,3968]{1,0:T(8,128)(2,1)}, bf16[192,3968]{1,0:T(8,128)(2,1)S(1)}, u32[]{:S(2)}, u32[]{:S(2)}) %collective-permute-start) | collective-permute-done | bytes 1523744 | tf_op jit(solution)/shard_map/while/body/eval_jaxpr/ppermute | solution.py:12
  685.2 2.0 conditional.2
  685.2 2.0 fusion.14
  688.3 2.0 dynamic_update_slice.15
  691.4 25.5 %collective-permute-done = bf16[192,3968]{1,0:T(8,128)(2,1)S(1)} collective-permute-done((bf16[192,3968]{1,0:T(8,128)(2,1)}, bf16[192,3968]{1,0:T(8,128)(2,1)S(1)}, u32[]{:S(2)}, u32[]{:S(2)}) %collective-permute-start) | collective-permute-done | bytes 1523744 | tf_op jit(solution)/shard_map/while/body/eval_jaxpr/ppermute | solution.py:12
  716.9 2.0 conditional.2
  716.9 2.0 fusion.14
  722.9 25.5 %collective-permute-done = bf16[192,3968]{1,0:T(8,128)(2,1)S(1)} collective-permute-done((bf16[192,3968]{1,0:T(8,128)(2,1)}, bf16[192,3968]{1,0:T(8,128)(2,1)S(1)}, u32[]{:S(2)}, u32[]{:S(2)}) %collective-permute-start) | collective-permute-done | bytes 1523744 | tf_op jit(solution)/shard_map/while/body/eval_jaxpr/ppermute | solution.py:12
  748.4 2.0 conditional.2
  748.4 2.0 fusion.14
  751.5 2.0 dynamic_update_slice.15
  754.6 25.5 %collective-permute-done = bf16[192,3968]{1,0:T(8,128)(2,1)S(1)} collective-permute-done((bf16[192,3968]{1,0:T(8,128)(2,1)}, bf16[192,3968]{1,0:T(8,128)(2,1)S(1)}, u32[]{:S(2)}, u32[]{:S(2)}) %collective-permute-start) | collective-permute-done | bytes 1523744 | tf_op jit(solution)/shard_map/while/body/eval_jaxpr/ppermute | solution.py:12
  780.1 2.0 conditional.2
  780.1 2.0 fusion.14
  786.1 25.5 %collective-permute-done = bf16[192,3968]{1,0:T(8,128)(2,1)S(1)} collective-permute-done((bf16[192,3968]{1,0:T(8,128)(2,1)}, bf16[192,3968]{1,0:T(8,128)(2,1)S(1)}, u32[]{:S(2)}, u32[]{:S(2)}) %collective-permute-start) | collective-permute-done | bytes 1523744 | tf_op jit(solution)/shard_map/while/body/eval_jaxpr/ppermute | solution.py:12
  811.6 2.0 conditional.2
  811.6 2.0 fusion.14
  814.7 2.0 dynamic_update_slice.15
  817.8 3.5 select_bitcast_fusion
  (86 shorter events, 53.8 us)
Async XLA Ops:
  0.0 10.8 %copy-start = (bf16[192,2048]{1,0:T(8,128)(2,1)S(1)}, bf16[192,2048]{1,0:T(8,128)(2,1)}, u32[]{:S(2)}) copy-start(bf16[192,2048]{1,0:T(8,128)(2,1)} %param.7) | copy-start | bytes 2359300
  1.8 14.6 %all-to-all-start = ((bf16[1,32,1]{2,0,1:T(2,128)(2,1)}), bf16[1,32,1]{2,0,1:T(2,128)(2,1)S(1)}, u32[]{:S(2)}, u32[]{:S(2)}) async-start(bf16[1,32,1]{2,0,1:T(2,128)(2,1)} %copy.14), calls=%async_computation | async-start | bytes 32768 | tf_op jit(solution)/shard_map/all_to_all | solution.py:50
  13.3 9.6 %copy-start.2 = (u32[256]{0:T(256)S(1)}, u32[256]{0:T(256)}, u32[]{:S(2)}) copy-start(u32[256]{0:T(256)} %constant.130) | copy-start | bytes 3076
  16.3 39.5 %all-to-all-start.1 = ((bf16[192,32,128]{2,0,1:T(8,128)(2,1)}), bf16[192,32,128]{2,0,1:T(8,128)(2,1)}, u32[]{:S(2)}, u32[]{:S(2)}) async-start(bf16[192,32,128]{2,0,1:T(8,128)(2,1)} %select_bitcast_fusion.1), calls=%async_computation.1 | async-start | bytes 3145728 | tf_op jit(solution)/shard_map/all_to_all | solution.py:49
  59.9 1.7 copy-start.1
  153.7 41.9 %collective-permute-start = (bf16[192,3968]{1,0:T(8,128)(2,1)}, bf16[192,3968]{1,0:T(8,128)(2,1)S(1)}, u32[]{:S(2)}, u32[]{:S(2)}) collective-permute-start(bf16[192,3968]{1,0:T(8,128)(2,1)} %get-tuple-element.215), channel_id=1, source_target_pairs={{0,1},{1,2},{2,3},{3,4},{4,5},{5,6},{6,7},{7,8},{8,9},{9,10},{10,1... | collective-permute-start | bytes 4571144 | tf_op jit(solution)/shard_map/while/body/eval_jaxpr/ppermute | solution.py:12
  201.6 42.3 %collective-permute-start = (bf16[192,3968]{1,0:T(8,128)(2,1)}, bf16[192,3968]{1,0:T(8,128)(2,1)S(1)}, u32[]{:S(2)}, u32[]{:S(2)}) collective-permute-start(bf16[192,3968]{1,0:T(8,128)(2,1)} %get-tuple-element.215), channel_id=1, source_target_pairs={{0,1},{1,2},{2,3},{3,4},{4,5},{5,6},{6,7},{7,8},{8,9},{9,10},{10,1... | collective-permute-start | bytes 4571144 | tf_op jit(solution)/shard_map/while/body/eval_jaxpr/ppermute | solution.py:12
  249.8 47.1 %collective-permute-start = (bf16[192,3968]{1,0:T(8,128)(2,1)}, bf16[192,3968]{1,0:T(8,128)(2,1)S(1)}, u32[]{:S(2)}, u32[]{:S(2)}) collective-permute-start(bf16[192,3968]{1,0:T(8,128)(2,1)} %get-tuple-element.215), channel_id=1, source_target_pairs={{0,1},{1,2},{2,3},{3,4},{4,5},{5,6},{6,7},{7,8},{8,9},{9,10},{10,1... | collective-permute-start | bytes 4571144 | tf_op jit(solution)/shard_map/while/body/eval_jaxpr/ppermute | solution.py:12
  303.1 43.3 %collective-permute-start = (bf16[192,3968]{1,0:T(8,128)(2,1)}, bf16[192,3968]{1,0:T(8,128)(2,1)S(1)}, u32[]{:S(2)}, u32[]{:S(2)}) collective-permute-start(bf16[192,3968]{1,0:T(8,128)(2,1)} %get-tuple-element.215), channel_id=1, source_target_pairs={{0,1},{1,2},{2,3},{3,4},{4,5},{5,6},{6,7},{7,8},{8,9},{9,10},{10,1... | collective-permute-start | bytes 4571144 | tf_op jit(solution)/shard_map/while/body/eval_jaxpr/ppermute | solution.py:12
  352.3 45.7 %collective-permute-start = (bf16[192,3968]{1,0:T(8,128)(2,1)}, bf16[192,3968]{1,0:T(8,128)(2,1)S(1)}, u32[]{:S(2)}, u32[]{:S(2)}) collective-permute-start(bf16[192,3968]{1,0:T(8,128)(2,1)} %get-tuple-element.215), channel_id=1, source_target_pairs={{0,1},{1,2},{2,3},{3,4},{4,5},{5,6},{6,7},{7,8},{8,9},{9,10},{10,1... | collective-permute-start | bytes 4571144 | tf_op jit(solution)/shard_map/while/body/eval_jaxpr/ppermute | solution.py:12
  404.2 43.3 %collective-permute-start = (bf16[192,3968]{1,0:T(8,128)(2,1)}, bf16[192,3968]{1,0:T(8,128)(2,1)S(1)}, u32[]{:S(2)}, u32[]{:S(2)}) collective-permute-start(bf16[192,3968]{1,0:T(8,128)(2,1)} %get-tuple-element.215), channel_id=1, source_target_pairs={{0,1},{1,2},{2,3},{3,4},{4,5},{5,6},{6,7},{7,8},{8,9},{9,10},{10,1... | collective-permute-start | bytes 4571144 | tf_op jit(solution)/shard_map/while/body/eval_jaxpr/ppermute | solution.py:12
  453.5 45.7 %collective-permute-start = (bf16[192,3968]{1,0:T(8,128)(2,1)}, bf16[192,3968]{1,0:T(8,128)(2,1)S(1)}, u32[]{:S(2)}, u32[]{:S(2)}) collective-permute-start(bf16[192,3968]{1,0:T(8,128)(2,1)} %get-tuple-element.215), channel_id=1, source_target_pairs={{0,1},{1,2},{2,3},{3,4},{4,5},{5,6},{6,7},{7,8},{8,9},{9,10},{10,1... | collective-permute-start | bytes 4571144 | tf_op jit(solution)/shard_map/while/body/eval_jaxpr/ppermute | solution.py:12
  505.4 43.3 %collective-permute-start = (bf16[192,3968]{1,0:T(8,128)(2,1)}, bf16[192,3968]{1,0:T(8,128)(2,1)S(1)}, u32[]{:S(2)}, u32[]{:S(2)}) collective-permute-start(bf16[192,3968]{1,0:T(8,128)(2,1)} %get-tuple-element.215), channel_id=1, source_target_pairs={{0,1},{1,2},{2,3},{3,4},{4,5},{5,6},{6,7},{7,8},{8,9},{9,10},{10,1... | collective-permute-start | bytes 4571144 | tf_op jit(solution)/shard_map/while/body/eval_jaxpr/ppermute | solution.py:12
  554.6 45.7 %collective-permute-start = (bf16[192,3968]{1,0:T(8,128)(2,1)}, bf16[192,3968]{1,0:T(8,128)(2,1)S(1)}, u32[]{:S(2)}, u32[]{:S(2)}) collective-permute-start(bf16[192,3968]{1,0:T(8,128)(2,1)} %get-tuple-element.215), channel_id=1, source_target_pairs={{0,1},{1,2},{2,3},{3,4},{4,5},{5,6},{6,7},{7,8},{8,9},{9,10},{10,1... | collective-permute-start | bytes 4571144 | tf_op jit(solution)/shard_map/while/body/eval_jaxpr/ppermute | solution.py:12
  606.6 43.3 %collective-permute-start = (bf16[192,3968]{1,0:T(8,128)(2,1)}, bf16[192,3968]{1,0:T(8,128)(2,1)S(1)}, u32[]{:S(2)}, u32[]{:S(2)}) collective-permute-start(bf16[192,3968]{1,0:T(8,128)(2,1)} %get-tuple-element.215), channel_id=1, source_target_pairs={{0,1},{1,2},{2,3},{3,4},{4,5},{5,6},{6,7},{7,8},{8,9},{9,10},{10,1... | collective-permute-start | bytes 4571144 | tf_op jit(solution)/shard_map/while/body/eval_jaxpr/ppermute | solution.py:12
  655.8 29.4 %collective-permute-start = (bf16[192,3968]{1,0:T(8,128)(2,1)}, bf16[192,3968]{1,0:T(8,128)(2,1)S(1)}, u32[]{:S(2)}, u32[]{:S(2)}) collective-permute-start(bf16[192,3968]{1,0:T(8,128)(2,1)} %get-tuple-element.215), channel_id=1, source_target_pairs={{0,1},{1,2},{2,3},{3,4},{4,5},{5,6},{6,7},{7,8},{8,9},{9,10},{10,1... | collective-permute-start | bytes 4571144 | tf_op jit(solution)/shard_map/while/body/eval_jaxpr/ppermute | solution.py:12
  691.4 25.5 %collective-permute-start = (bf16[192,3968]{1,0:T(8,128)(2,1)}, bf16[192,3968]{1,0:T(8,128)(2,1)S(1)}, u32[]{:S(2)}, u32[]{:S(2)}) collective-permute-start(bf16[192,3968]{1,0:T(8,128)(2,1)} %get-tuple-element.215), channel_id=1, source_target_pairs={{0,1},{1,2},{2,3},{3,4},{4,5},{5,6},{6,7},{7,8},{8,9},{9,10},{10,1... | collective-permute-start | bytes 4571144 | tf_op jit(solution)/shard_map/while/body/eval_jaxpr/ppermute | solution.py:12
  722.9 25.5 %collective-permute-start = (bf16[192,3968]{1,0:T(8,128)(2,1)}, bf16[192,3968]{1,0:T(8,128)(2,1)S(1)}, u32[]{:S(2)}, u32[]{:S(2)}) collective-permute-start(bf16[192,3968]{1,0:T(8,128)(2,1)} %get-tuple-element.215), channel_id=1, source_target_pairs={{0,1},{1,2},{2,3},{3,4},{4,5},{5,6},{6,7},{7,8},{8,9},{9,10},{10,1... | collective-permute-start | bytes 4571144 | tf_op jit(solution)/shard_map/while/body/eval_jaxpr/ppermute | solution.py:12
  754.6 25.5 %collective-permute-start = (bf16[192,3968]{1,0:T(8,128)(2,1)}, bf16[192,3968]{1,0:T(8,128)(2,1)S(1)}, u32[]{:S(2)}, u32[]{:S(2)}) collective-permute-start(bf16[192,3968]{1,0:T(8,128)(2,1)} %get-tuple-element.215), channel_id=1, source_target_pairs={{0,1},{1,2},{2,3},{3,4},{4,5},{5,6},{6,7},{7,8},{8,9},{9,10},{10,1... | collective-permute-start | bytes 4571144 | tf_op jit(solution)/shard_map/while/body/eval_jaxpr/ppermute | solution.py:12
  786.1 25.5 %collective-permute-start = (bf16[192,3968]{1,0:T(8,128)(2,1)}, bf16[192,3968]{1,0:T(8,128)(2,1)S(1)}, u32[]{:S(2)}, u32[]{:S(2)}) collective-permute-start(bf16[192,3968]{1,0:T(8,128)(2,1)} %get-tuple-element.215), channel_id=1, source_target_pairs={{0,1},{1,2},{2,3},{3,4},{4,5},{5,6},{6,7},{7,8},{8,9},{9,10},{10,1... | collective-permute-start | bytes 4571144 | tf_op jit(solution)/shard_map/while/body/eval_jaxpr/ppermute | solution.py:12
where the time goes:
time: 823 us; the launch traced here: 821 us
  waiting for transfers between devices  606 us (74%)
  blocking collectives  88.5 us (11%)
  local copies, waits for them, and re-layouts  54.5 us (7%)
  matrix products  30.2 us (4%)
  other arithmetic  25.3 us (3%)
  starting transfers between devices  15.5 us (2%)
    ppermute x15, waiting for transfers between devices, from_behind(): return lax.ppermute(x, axis, [(i, (i + by) % count) for i in range(count)])  573 us
    unnamed x1, blocking collectives  88.5 us
    dot_general x16, matrix products, gram(): lax.dot_general(left, right, (((1,), (1,)), ((), ())), preferred_element_...  30.2 us
    all_to_all x1, waiting for transfers between devices, on_device(): lax.all_to_all(outgoing, 'blk', split_axis=1, concat_axis=1, tiled=True)  29.4 us
    dynamic_update_slice x15, local copies, waits for them, and re-layouts, visit(): lax.dynamic_update_slice(total, jnp.where(keep, tile, held), (0, offset))  27.8 us
    while x15, local copies, waits for them, and re-layouts  16.8 us
  transfers between devices with their start and end apart: 17, of which 17 were waited for; matrix products, arithmetic and copies ran while one was open for 1% of the time, Pallas kernels for 0%

commit v1 on v0

v1 whole, which is shorter than its diff:
```python
import functools

import jax
import jax.numpy as jnp
from jax import lax
from jax.experimental import pallas as pl
from jax.experimental.pallas import tpu as pltpu
from jax.sharding import PartitionSpec as P

BLOCK = 128
MESH = pl.DeviceIdType.MESH
NY = 4
W = 2 * BLOCK


def prep_kernel(bc_ref, order_ref, x_ref, o_ref):
    blk_dev = x_ref.shape[1] // BLOCK

    def one(s, carry):
        cyc = order_ref[s]
        first = jnp.int32(-1)
        second = jnp.int32(-1)
        for j in range(blk_dev):
            hit = bc_ref[j] == cyc
            second = jnp.where(jnp.logical_and(hit, first >= 0), j, second)
            first = jnp.where(jnp.logical_and(hit, first < 0), j, first)
        for r, src in ((0, first), (1, second)):
            cols = pl.ds(r * BLOCK, BLOCK)

            @pl.when(src >= 0)
            def _():
                start = pl.multiple_of(src * BLOCK, BLOCK)
                o_ref[s, :, cols] = x_ref[:, pl.ds(start, BLOCK)]

            @pl.when(src < 0)
            def _():
                o_ref[s, :, cols] = jnp.zeros((x_ref.shape[0], BLOCK), x_ref.dtype)

        return carry

    lax.fori_loop(0, order_ref.shape[0], one, 0)


def dot_t(a, b):
    return lax.dot_general(a, b, (((1,), (1,)), ((), ())), preferred_element_type=jnp.float32)


def main_kernel(
    out_ref, gram_ref, s_ref,
    a_buf, o_buf, cs, cx, rs, rx, tsum, ret,
    st_send, st_recv, y_send, y_recv, c_send, c_recv, t_send, t_recv, s_send, s_recv,
):
    nblk, panel, _ = out_ref.shape
    nsrc = nblk // 2
    b = lax.axis_index("blk")
    t = lax.axis_index("tm")
    c = t % 2
    h = (t // 2) % 2
    y = t // 4
    bp = b % 2
    bm = b // 2
    half = 2 * panel

    def tm_of(yy, hh, cc):
        return (yy * 2 + hh) * 2 + cc

    other = (b, tm_of(y, h, 1 - c))

    barrier = pltpu.get_barrier_semaphore()

    def greet(k, carry):
        s = (b + k) % nblk
        for j in range(4):
            pl.semaphore_signal(barrier, inc=1, device_id=(s, y * 4 + j), device_id_type=MESH)
        return carry

    lax.fori_loop(1, nblk, greet, 0)
    for j in range(1, 4):
        pl.semaphore_signal(barrier, inc=1, device_id=(b, y * 4 + (t + j) % 4), device_id_type=MESH)
    for r in range(1, NY):
        for q in range(2):
            pl.semaphore_signal(
                barrier, inc=1, device_id=(b, tm_of((y + r) % NY, h, q)), device_id_type=MESH
            )
    pl.semaphore_wait(barrier, (nblk - 1) * 4 + 3 + (NY - 1) * 2)

    my_rows = pl.ds(pl.multiple_of(c * panel, panel), panel)
    my_cols = pl.ds(pl.multiple_of(bm * W, W), W)

    def st_copy(k, d):
        s = (b + k) % nblk
        dst = a_buf.at[y, my_rows, my_cols] if d == 0 else o_buf.at[my_rows, my_cols]
        return pltpu.make_async_remote_copy(
            src_ref=out_ref.at[s],
            dst_ref=dst,
            send_sem=st_send.at[d, k],
            recv_sem=st_recv.at[d, bm, c],
            device_id=(s, tm_of(y, h if d == 0 else 1 - h, bp)),
            device_id_type=MESH,
        )

    def local_copy():
        return pltpu.make_async_copy(
            out_ref.at[b], a_buf.at[y, my_rows, my_cols], st_recv.at[0, bm, c]
        )

    st_copy(0, 1).start()

    @pl.when(bp == c)
    def _():
        local_copy().start()

    @pl.when(bp != c)
    def _():
        st_copy(0, 0).start()

    def send_one(k, carry):
        for d in range(2):
            st_copy(k, d).start()
        return carry

    lax.fori_loop(1, nblk, send_one, 0)

    def st_wait(d, m, q):
        rows = pl.ds(q * panel, panel)
        cols = pl.ds(pl.multiple_of(m * W, W), W)
        dst = a_buf.at[y, rows, cols] if d == 0 else o_buf.at[rows, cols]
        pltpu.make_async_remote_copy(
            src_ref=out_ref.at[0], dst_ref=dst, send_sem=st_send.at[d, 0], recv_sem=st_recv.at[d, m, q],
            device_id=other, device_id_type=MESH,
        ).wait_recv()

    def y_copy(m, r, src_y, to_y):
        cols = pl.ds(pl.multiple_of(m * W, W), W)
        return pltpu.make_async_remote_copy(
            src_ref=a_buf.at[src_y, :, cols],
            dst_ref=a_buf.at[src_y, :, cols],
            send_sem=y_send.at[m, r],
            recv_sem=y_recv.at[m, r],
            device_id=(b, tm_of(to_y, h, c)),
            device_id_type=MESH,
        )

    def forward(m, carry):
        for q in range(2):
            st_wait(0, m, q)
        for r in range(1, NY):
            y_copy(m, r, y, (y + r) % NY).start()
        return carry

    lax.fori_loop(0, nsrc, forward, 0)

    def wait_other(m, carry):
        for q in range(2):
            st_wait(1, m, q)
        return carry

    lax.fori_loop(0, nsrc, wait_other, 0)

    ones = jnp.ones((8, nsrc * W), jnp.bfloat16)
    own_sum = dot_t(ones, a_buf[y])
    oth_sum = dot_t(ones, o_buf[...])
    head = a_buf[y, 0:16, :].astype(jnp.float32)
    lane = lax.broadcasted_iota(jnp.int32, head.shape, 1)
    row = lax.broadcasted_iota(jnp.int32, head.shape, 0)
    mark = jnp.where(jnp.logical_and(lane % BLOCK == 0, row == 0), head, 0.0)
    filled = jnp.sum(jnp.where(mark > 0.0, 1.0, 0.0))
    srow = lax.broadcasted_iota(jnp.int32, (8, half), 0)
    s_ref[c, y, :, pl.ds(pl.multiple_of(h * half, half), half)] = jnp.where(srow == 1, filled, own_sum)
    s_ref[c, y, :, pl.ds(pl.multiple_of((1 - h) * half, half), half)] = jnp.where(srow == 1, filled, oth_sum)

    def s_copy(r, q, cc, yy, to):
        return pltpu.make_async_remote_copy(
            src_ref=s_ref.at[cc, yy], dst_ref=s_ref.at[cc, yy],
            send_sem=s_send.at[r, q], recv_sem=s_recv.at[r, q],
            device_id=to, device_id_type=MESH,
        )

    for r in range(NY):
        for q in range(2):
            if r == 0 and q == 0:
                continue
            cc = c if q == 0 else 1 - c
            s_copy(r, q, c, y, (b, tm_of((y + r) % NY, h, cc))).start()

    def wait_y(m, carry):
        for r in range(1, NY):
            y_copy(m, r, (y - r + NY) % NY, y).wait_recv()
        return carry

    lax.fori_loop(0, nsrc, wait_y, 0)

    theirs = pl.ds(pl.multiple_of((1 - c) * panel, panel), panel)
    mine = pl.ds(pl.multiple_of(c * panel, panel), panel)

    def c_copy(kind, u):
        src, dst = (cs, rs) if kind == 0 else (cx, rx)
        return pltpu.make_async_remote_copy(
            src_ref=src.at[u, theirs, :], dst_ref=dst.at[u],
            send_sem=c_send.at[kind, u], recv_sem=c_recv.at[kind, u],
            device_id=other, device_id_type=MESH,
        )

    def t_copy(yy, u):
        return pltpu.make_async_remote_copy(
            src_ref=tsum.at[u], dst_ref=ret.at[yy],
            send_sem=t_send.at[u], recv_sem=t_recv.at[yy],
            device_id=(b, tm_of(u, h, c)), device_id_type=MESH,
        )

    def cross(u, carry):
        @pl.when(u <= y)
        def _():
            cx[u] = dot_t(a_buf[u], o_buf[...])
            c_copy(1, u).start()
        return carry

    lax.fori_loop(0, NY, cross, 0)

    def same(u, carry):
        @pl.when(u >= y)
        def _():
            cs[u] = dot_t(a_buf[y], a_buf[u])
            c_copy(0, u).start()
        return carry

    lax.fori_loop(0, NY, same, 0)

    def combine(u, carry):
        @pl.when(u <= y)
        def _():
            c_copy(1, u).wait_recv()
            tsum[u] = cx[u, mine, :] + rx[u]

        @pl.when(u < y)
        def _():
            t_copy(y, u).start()
        return carry

    lax.fori_loop(0, NY, combine, 0)

    def place(u, carry):
        same_cols = pl.ds(pl.multiple_of(u * 2 * half + h * half, half), half)
        cross_cols = pl.ds(pl.multiple_of(u * 2 * half + (1 - h) * half, half), half)

        @pl.when(u < y)
        def _():
            gram_ref[:, same_cols] = jnp.zeros((panel, half), jnp.float32)
            gram_ref[:, cross_cols] = jnp.zeros((panel, half), jnp.float32)

        @pl.when(u >= y)
        def _():
            c_copy(0, u).wait_recv()
            gram_ref[:, same_cols] = cs[u, mine, :] + rs[u]

        @pl.when(u == y)
        def _():
            gram_ref[:, cross_cols] = tsum[u]

        @pl.when(u > y)
        def _():
            t_copy(u, y).wait_recv()
            gram_ref[:, cross_cols] = ret[u]
        return carry

    lax.fori_loop(0, NY, place, 0)

    for r in range(NY):
        for q in range(2):
            if r == 0 and q == 0:
                continue
            cc = c if q == 0 else 1 - c
            s_copy(r, q, cc, (y - r + NY) % NY, other).wait_recv()

    st_copy(0, 1).wait_send()

    @pl.when(bp != c)
    def _():
        st_copy(0, 0).wait_send()

    def drain_one(k, carry):
        for d in range(2):
            st_copy(k, d).wait_send()
        return carry

    lax.fori_loop(1, nblk, drain_one, 0)

    def drain_y(m, carry):
        for r in range(1, NY):
            y_copy(m, r, y, (y + r) % NY).wait_send()
        return carry

    lax.fori_loop(0, nsrc, drain_y, 0)

    def drain_c(u, carry):
        @pl.when(u <= y)
        def _():
            c_copy(1, u).wait_send()

        @pl.when(u >= y)
        def _():
            c_copy(0, u).wait_send()

        @pl.when(u < y)
        def _():
            t_copy(y, u).wait_send()
        return carry

    lax.fori_loop(0, NY, drain_c, 0)
    for r in range(NY):
        for q in range(2):
            if r == 0 and q == 0:
                continue
            s_copy(r, q, c, y, other).wait_send()


def on_device(intensity, block_cycle, cycle_order):
    panel = intensity.shape[0]
    nblk = cycle_order.shape[0]
    nsrc = nblk // 2
    half = 2 * panel
    frames = panel * lax.axis_size("tm")
    vmem = pl.BlockSpec(memory_space=pltpu.VMEM)
    smem = pl.BlockSpec(memory_space=pltpu.SMEM)
    outgoing = pl.pallas_call(
        prep_kernel,
        out_shape=jax.ShapeDtypeStruct((nblk, panel, W), jnp.bfloat16),
        in_specs=[smem, smem, vmem],
        out_specs=vmem,
        name="prep",
    )(block_cycle, cycle_order, intensity)
    dma = pltpu.SemaphoreType.DMA
    gram, parts = pl.pallas_call(
        main_kernel,
        out_shape=(
            jax.ShapeDtypeStruct((panel, frames), jnp.float32),
            jax.ShapeDtypeStruct((2, NY, 8, 2 * half), jnp.float32),
        ),
        in_specs=[vmem],
        out_specs=(vmem, vmem),
        scratch_shapes=[
            pltpu.VMEM((NY, half, nsrc * W), jnp.bfloat16),
            pltpu.VMEM((half, nsrc * W), jnp.bfloat16),
            pltpu.VMEM((NY, half, half), jnp.float32),
            pltpu.VMEM((NY, half, half), jnp.float32),
            pltpu.VMEM((NY, panel, half), jnp.float32),
            pltpu.VMEM((NY, panel, half), jnp.float32),
            pltpu.VMEM((NY, panel, half), jnp.float32),
            pltpu.VMEM((NY, panel, half), jnp.float32),
            dma((2, nblk)), dma((2, nsrc, 2)),
            dma((nsrc, NY)), dma((nsrc, NY)),
            dma((2, NY)), dma((2, NY)),
            dma((NY,)), dma((NY,)),
            dma((NY, 2)), dma((NY, 2)),
        ],
        compiler_params=pltpu.CompilerParams(
            collective_id=0, has_side_effects=True, vmem_limit_bytes=56 << 20
        ),
        name="exchange",
    )(outgoing)
    me = lax.axis_index("tm")
    y = me // 4
    sums = (parts[0, :, 0, :] + parts[1, :, 0, :]).reshape(frames)
    count = (parts[0, 0, 1, 0] + parts[1, 0, 1, 0]) * BLOCK
    own = lax.dynamic_slice(sums, (me * panel,), (panel,))
    column_panel = jnp.arange(frames, dtype=jnp.int32) // panel
    scaled = gram * count / (own[:, None] * sums[None, :])
    twotime = jnp.where((column_panel >= me)[None, :], scaled, jnp.float32(0.0))
    return twotime.reshape(1, panel, frames)


def solution(mesh):
    placed = (P("tm", "blk"), P("blk"), P())
    return jax.shard_map(
        on_device, mesh=mesh, in_specs=placed, out_specs=P("blk", "tm", None), check_vma=False
    )
```

time: 823 us -> 180 us (0.22)
  the two profiles are of different devices: /device:TPU:4 before, /device:TPU:103 now
where the time goes in v1:
time: 180 us; the launch traced here: 179 us
  Pallas kernels  172 us (96%)
  other arithmetic  4.5 us (2%)
    pallas_call x1, Pallas kernels, on_device(): pl.pallas_call(main_kernel, out_shape=(jax.ShapeDtypeStruct((panel, frame...  169 us
    pallas_call x1, Pallas kernels, on_device(): pl.pallas_call(prep_kernel, out_shape=jax.ShapeDtypeStruct((nblk, panel,...  3.66 us

profile of v1, /device:TPU:103, one launch (start us, length us, event | category | flops | bytes accessed | tf_op | source)
XLA Modules:
  0.0 179.5 jit_solution(3759689888281503083)
XLA Ops:
  0.0 3.7 %prep.1.out_ref = bf16[16,192,256]{2,1,0:T(8,128)(2,1)} custom-call(s32[16]{0:T(128)} %bc_ref.1, s32[16]{0:T(128)} %order_ref.1, bf16[192,2048]{1,0:T(8,128)(2,1)} %x_ref.1), custom_call_target="tpu_custom_call" | custom-call | tf_op jit(solution)/shard_map/prep/pallas_call | solution.py:325
  3.7 168.8 %exchange.1 = (f32[192,3072]{1,0:T(8,128)}, f32[2,4,8,768]{3,2,1,0:T(8,128)}) custom-call(bf16[16,192,256]{2,1,0:T(8,128)(2,1)} %prep.1.out_ref), custom_call_target="tpu_custom_call" | custom-call | tf_op jit(solution)/shard_map/exchange/pallas_call | solution.py:333
  172.5 1.2 fusion.4
  174.9 1.0 slice_add_fusion
  175.9 0.1 dynamic_slice.3
  175.9 3.5 %select_bitcast_fusion = f32[1,192,3072]{2,1,0:T(8,128)} fusion(f32[192,3072]{1,0:T(8,128)} %get-tuple-element.7, f32[3072]{0:T(1024)S(1)} %bitcast.5, f32[192]{0:T(256)S(1)} %dynamic_slice.3, f32[]{:T(128)} %bitcast, pred[3072]{0:T(1024)(128)(4,1)S(1)} %fusion), kind=kLoop, calls=%fused_computation | loop fusion | flops 2359296 | bytes 4734724 | tf_op jit(solution)/shard_map/reshape | solution.py:369
  (1 shorter events, 0.0 us)

commit v2 on v1

v2 whole, which is shorter than its diff:
```python
import jax
import jax.numpy as jnp
from jax import lax
from jax.experimental import pallas as pl
from jax.experimental.pallas import tpu as pltpu
from jax.sharding import PartitionSpec as P

BLOCK = 128
MESH = pl.DeviceIdType.MESH
NY = 4
W = 2 * BLOCK


def dot_t(a, b):
    return lax.dot_general(a, b, (((1,), (1,)), ((), ())), preferred_element_type=jnp.float32)


def main_kernel(
    bc_ref, order_ref, x_ref, out_ref,
    slots, a_buf, o_buf, acc_s, acc_x, rs, rx, tsum, sum_acc, s_mine, s_oth, s_tot, s_col,
    st_send, st_recv, y_send, y_recv, c_send, c_recv, t_send, t_recv, s_send, s_recv,
):
    nblk, panel, _ = slots.shape
    nsrc = nblk // 2
    b = lax.axis_index("blk")
    t = lax.axis_index("tm")
    c = t % 2
    h = (t // 2) % 2
    y = t // 4
    bp = b % 2
    bm = b // 2
    half = 2 * panel
    up = (y + 1) % NY
    down = (y + NY - 1) % NY
    far = (y + 2) % NY

    def tm_of(yy, hh, cc):
        return (yy * 2 + hh) * 2 + cc

    other = (b, tm_of(y, h, 1 - c))

    barrier = pltpu.get_barrier_semaphore()

    def greet(k, carry):
        s = (b + k) % nblk
        for j in range(4):
            pl.semaphore_signal(barrier, inc=1, device_id=(s, y * 4 + j), device_id_type=MESH)
        return carry

    lax.fori_loop(1, nblk, greet, 0)
    for j in range(1, 4):
        pl.semaphore_signal(barrier, inc=1, device_id=(b, y * 4 + (t + j) % 4), device_id_type=MESH)
    for r in range(1, NY):
        pl.semaphore_signal(
            barrier, inc=1, device_id=(b, tm_of((y + r) % NY, h, c)), device_id_type=MESH
        )

    blk_dev = x_ref.shape[1] // BLOCK

    def fill(s, carry):
        cyc = order_ref[s]
        first = jnp.int32(-1)
        second = jnp.int32(-1)
        for j in range(blk_dev):
            hit = bc_ref[j] == cyc
            second = jnp.where(jnp.logical_and(hit, first >= 0), j, second)
            first = jnp.where(jnp.logical_and(hit, first < 0), j, first)
        for r, src in ((0, first), (1, second)):
            start = jnp.maximum(src, 0) * BLOCK
            keep = jnp.where(src >= 0, jnp.float32(1.0), jnp.float32(0.0))
            block = x_ref[:, pl.ds(start, BLOCK)].astype(jnp.float32) * keep
            slots[s, :, pl.ds(r * BLOCK, BLOCK)] = block.astype(jnp.bfloat16)
        return carry

    lax.fori_loop(0, nblk, fill, 0)

    def clear(u, carry):
        acc_s[u] = jnp.zeros((half, half), jnp.float32)
        acc_x[u] = jnp.zeros((half, half), jnp.float32)
        return carry

    lax.fori_loop(0, NY, clear, 0)
    sum_acc[...] = jnp.zeros(sum_acc.shape, jnp.float32)

    pl.semaphore_wait(barrier, (nblk - 1) * 4 + 3 + (NY - 1))

    my_rows = pl.ds(pl.multiple_of(c * panel, panel), panel)
    my_cols = pl.ds(pl.multiple_of(bm * W, W), W)

    def st_copy(k, d):
        s = (b + k) % nblk
        dst = a_buf.at[y, my_rows, my_cols] if d == 0 else o_buf.at[my_rows, my_cols]
        return pltpu.make_async_remote_copy(
            src_ref=slots.at[s],
            dst_ref=dst,
            send_sem=st_send.at[d, k],
            recv_sem=st_recv.at[d, bm, c],
            device_id=(s, tm_of(y, h if d == 0 else 1 - h, bp)),
            device_id_type=MESH,
        )

    st_copy(0, 1).start()

    @pl.when(bp == c)
    def _():
        pltpu.make_async_copy(
            slots.at[b], a_buf.at[y, my_rows, my_cols], st_recv.at[0, bm, c]
        ).start()

    @pl.when(bp != c)
    def _():
        st_copy(0, 0).start()

    def send_one(k, carry):
        for d in range(2):
            st_copy(k, d).start()
        return carry

    lax.fori_loop(1, nblk, send_one, 0)

    def st_wait(d, m, q):
        rows = pl.ds(q * panel, panel)
        cols = pl.ds(pl.multiple_of(m * W, W), W)
        dst = a_buf.at[y, rows, cols] if d == 0 else o_buf.at[rows, cols]
        pltpu.make_async_remote_copy(
            src_ref=slots.at[0], dst_ref=dst, send_sem=st_send.at[d, 0], recv_sem=st_recv.at[d, m, q],
            device_id=other, device_id_type=MESH,
        ).wait_recv()

    whole = pl.ds(0, half)
    low = pl.ds(0, panel)
    high = pl.ds(panel, panel)

    def y_copy(m, way, src_y, rows, to_y):
        cols = pl.ds(pl.multiple_of(m * W, W), W)
        return pltpu.make_async_remote_copy(
            src_ref=a_buf.at[src_y, rows, cols],
            dst_ref=a_buf.at[src_y, rows, cols],
            send_sem=y_send.at[m, way],
            recv_sem=y_recv.at[m, way],
            device_id=(b, tm_of(to_y, h, c)),
            device_id_type=MESH,
        )

    def source(j):
        k = 2 * j + (b + c) % 2
        return ((b + nblk - k) % nblk) // 2

    ones = jnp.ones((8, W), jnp.bfloat16)

    def multiply(m):
        cols = pl.ds(pl.multiple_of(m * W, W), W)

        def job(u, carry):
            panel_u = a_buf[u, :, cols]
            sum_acc[u] += dot_t(ones, panel_u)

            @pl.when(u <= y)
            def _():
                acc_x[u] += dot_t(panel_u, o_buf[:, cols])

            @pl.when(u >= y)
            def _():
                acc_s[u] += dot_t(a_buf[y, :, cols], panel_u)
            return carry

        lax.fori_loop(0, NY, job, 0)
        sum_acc[NY] += dot_t(ones, o_buf[:, cols])

    def step(j, carry):
        @pl.when(j < nsrc)
        def _():
            m = source(j)
            for q in range(2):
                st_wait(0, m, q)
            y_copy(m, 0, y, whole, up).start()
            y_copy(m, 1, y, whole, down).start()

        @pl.when(jnp.logical_and(j >= 1, j < nsrc + 1))
        def _():
            m = source(j - 1)
            y_copy(m, 0, down, whole, y).wait_recv()
            y_copy(m, 2, down, low, up).start()
            y_copy(m, 1, up, whole, y).wait_recv()
            y_copy(m, 3, up, high, down).start()

        @pl.when(j >= 2)
        def _():
            m = source(j - 2)
            for q in range(2):
                st_wait(1, m, q)
            y_copy(m, 2, far, low, y).wait_recv()
            y_copy(m, 3, far, high, y).wait_recv()
            multiply(m)
        return carry

    lax.fori_loop(0, nsrc + 2, step, 0)

    theirs = pl.ds(pl.multiple_of((1 - c) * panel, panel), panel)
    mine = pl.ds(pl.multiple_of(c * panel, panel), panel)

    head = a_buf[y, 0:16, :].astype(jnp.float32)
    lane = lax.broadcasted_iota(jnp.int32, head.shape, 1)
    row = lax.broadcasted_iota(jnp.int32, head.shape, 0)
    mark = jnp.where(jnp.logical_and(lane % BLOCK == 0, row == 0), head, 0.0)
    filled = jnp.sum(jnp.where(mark > 0.0, 1.0, 0.0))
    srow = lax.broadcasted_iota(jnp.int32, sum_acc.shape, 1)
    s_mine[...] = jnp.where(srow == 1, filled, sum_acc[...])
    s_copy = pltpu.make_async_remote_copy(
        src_ref=s_mine, dst_ref=s_oth, send_sem=s_send, recv_sem=s_recv,
        device_id=other, device_id_type=MESH,
    )
    s_copy.start()

    def c_copy(kind, u):
        src, dst = (acc_s, rs) if kind == 0 else (acc_x, rx)
        return pltpu.make_async_remote_copy(
            src_ref=src.at[u, theirs, :], dst_ref=dst.at[u],
            send_sem=c_send.at[kind, u], recv_sem=c_recv.at[kind, u],
            device_id=other, device_id_type=MESH,
        )

    def t_copy(yy, u):
        cols = pl.ds(pl.multiple_of(yy * 2 * half + (1 - h) * half, half), half)
        return pltpu.make_async_remote_copy(
            src_ref=tsum.at[u], dst_ref=out_ref.at[:, cols],
            send_sem=t_send.at[u], recv_sem=t_recv.at[yy],
            device_id=(b, tm_of(u, h, c)), device_id_type=MESH,
        )

    def share_cross(u, carry):
        @pl.when(u <= y)
        def _():
            c_copy(1, u).start()
        return carry

    def share_same(u, carry):
        @pl.when(u >= y)
        def _():
            c_copy(0, u).start()
        return carry

    lax.fori_loop(0, NY, share_cross, 0)
    lax.fori_loop(0, NY, share_same, 0)

    s_copy.wait_recv()
    for u in range(NY + 1):
        total = s_mine[u] + s_oth[u]
        s_tot[u] = total
        s_col[u] = total.T
    count = s_tot[0, 1:2, 0:1] * BLOCK

    def scaled(g, u_row, u_col):
        si = s_col[u_row, mine, 0:1]
        sj = s_tot[u_col, 0:1, :]
        return g * count / (si * sj)

    def back(u, carry):
        @pl.when(u < y)
        def _():
            c_copy(1, u).wait_recv()
            tsum[u] = scaled(acc_x[u, mine, :] + rx[u], u, NY)
            t_copy(y, u).start()
        return carry

    lax.fori_loop(0, NY, back, 0)

    tile = lax.broadcasted_iota(jnp.int32, (panel, half), 1)

    def place(u, carry):
        same_cols = pl.ds(pl.multiple_of(u * 2 * half + h * half, half), half)
        cross_cols = pl.ds(pl.multiple_of(u * 2 * half + (1 - h) * half, half), half)

        @pl.when(u < y)
        def _():
            out_ref[:, same_cols] = jnp.zeros((panel, half), jnp.float32)
            out_ref[:, cross_cols] = jnp.zeros((panel, half), jnp.float32)

        @pl.when(u >= y)
        def _():
            c_copy(0, u).wait_recv()
            g = scaled(acc_s[u, mine, :] + rs[u], y, u)
            first_tile = u * 4 + h * 2
            tiles = first_tile + jnp.where(tile >= panel, 1, 0)
            out_ref[:, same_cols] = jnp.where(tiles >= t, g, 0.0)

        @pl.when(u == y)
        def _():
            c_copy(1, u).wait_recv()
            g = scaled(acc_x[u, mine, :] + rx[u], y, NY)
            first_tile = u * 4 + (1 - h) * 2
            tiles = first_tile + jnp.where(tile >= panel, 1, 0)
            out_ref[:, cross_cols] = jnp.where(tiles >= t, g, 0.0)
        return carry

    lax.fori_loop(0, NY, place, 0)

    def arrive(u, carry):
        @pl.when(u > y)
        def _():
            t_copy(u, y).wait_recv()
        return carry

    lax.fori_loop(0, NY, arrive, 0)

    st_copy(0, 1).wait_send()

    @pl.when(bp != c)
    def _():
        st_copy(0, 0).wait_send()

    def drain_one(k, carry):
        for d in range(2):
            st_copy(k, d).wait_send()
        return carry

    lax.fori_loop(1, nblk, drain_one, 0)

    def drain_y(m, carry):
        y_copy(m, 0, y, whole, up).wait_send()
        y_copy(m, 1, y, whole, down).wait_send()
        y_copy(m, 2, down, low, up).wait_send()
        y_copy(m, 3, up, high, down).wait_send()
        return carry

    lax.fori_loop(0, nsrc, drain_y, 0)

    def drain_c(u, carry):
        @pl.when(u <= y)
        def _():
            c_copy(1, u).wait_send()

        @pl.when(u >= y)
        def _():
            c_copy(0, u).wait_send()

        @pl.when(u < y)
        def _():
            t_copy(y, u).wait_send()
        return carry

    lax.fori_loop(0, NY, drain_c, 0)
    s_copy.wait_send()


def on_device(intensity, block_cycle, cycle_order):
    panel = intensity.shape[0]
    nblk = cycle_order.shape[0]
    nsrc = nblk // 2
    half = 2 * panel
    frames = panel * lax.axis_size("tm")
    vmem = pl.BlockSpec(memory_space=pltpu.VMEM)
    smem = pl.BlockSpec(memory_space=pltpu.SMEM)
    dma = pltpu.SemaphoreType.DMA
    twotime = pl.pallas_call(
        main_kernel,
        out_shape=jax.ShapeDtypeStruct((panel, frames), jnp.float32),
        in_specs=[smem, smem, vmem],
        out_specs=vmem,
        scratch_shapes=[
            pltpu.VMEM((nblk, panel, W), jnp.bfloat16),
            pltpu.VMEM((NY, half, nsrc * W), jnp.bfloat16),
            pltpu.VMEM((half, nsrc * W), jnp.bfloat16),
            pltpu.VMEM((NY, half, half), jnp.float32),
            pltpu.VMEM((NY, half, half), jnp.float32),
            pltpu.VMEM((NY, panel, half), jnp.float32),
            pltpu.VMEM((NY, panel, half), jnp.float32),
            pltpu.VMEM((NY, panel, half), jnp.float32),
            pltpu.VMEM((NY + 1, 8, half), jnp.float32),
            pltpu.VMEM((NY + 1, 8, half), jnp.float32),
            pltpu.VMEM((NY + 1, 8, half), jnp.float32),
            pltpu.VMEM((NY + 1, 8, half), jnp.float32),
            pltpu.VMEM((NY + 1, half, 8), jnp.float32),
            dma((2, nblk)), dma((2, nsrc, 2)),
            dma((nsrc, 4)), dma((nsrc, 4)),
            dma((2, NY)), dma((2, NY)),
            dma((NY,)), dma((NY,)),
            dma, dma,
        ],
        compiler_params=pltpu.CompilerParams(
            collective_id=0, has_side_effects=True, vmem_limit_bytes=56 << 20
        ),
        name="exchange",
    )(block_cycle, cycle_order, intensity)
    return twotime.reshape(1, panel, frames)


def solution(mesh):
    placed = (P("tm", "blk"), P("blk"), P())
    return jax.shard_map(
        on_device, mesh=mesh, in_specs=placed, out_specs=P("blk", "tm", None), check_vma=False
    )
```

time: 180 us -> 122 us (0.68)
  the two profiles are of different devices: /device:TPU:103 before, /device:TPU:1 now
where the time goes in v2:
time: 122 us; the launch traced here: 120 us
  Pallas kernels  117 us (96%)
  local copies, waits for them, and re-layouts  3.3 us (3%)
    pallas_call x1, Pallas kernels, on_device(): pl.pallas_call(main_kernel, out_shape=jax.ShapeDtypeStruct((panel, frames...  117 us
    unnamed x1, local copies, waits for them, and re-layouts  3.3 us

profile of v2, /device:TPU:1, one launch (start us, length us, event | category | flops | bytes accessed | tf_op | source)
XLA Modules:
  0.0 120.5 jit_solution(897883685431329407)
XLA Ops:
  0.0 117.2 %exchange.1 = f32[192,3072]{1,0:T(8,128)} custom-call(s32[16]{0:T(128)} %bc_ref.1, s32[16]{0:T(128)} %order_ref.1, bf16[192,2048]{1,0:T(8,128)(2,1)} %x_ref.1), custom_call_target="tpu_custom_call" | custom-call | tf_op jit(solution)/shard_map/exchange/pallas_call | solution.py:355
  117.2 3.3 %copy.5 = f32[1,192,3072]{2,1,0:T(8,128)} copy(f32[1,192,3072]{2,1,0:T(8,128)} %bitcast.1) | data formatting | bytes 4718592

commit v3 on v2

--- a/solution.py
+++ b/solution.py
@@ -9,6 +9,10 @@
 MESH = pl.DeviceIdType.MESH
 NY = 4
 W = 2 * BLOCK
+STRIDE = 7
+LAG = 1
+AHEAD = 2
+CUT = 2
 
 
 def dot_t(a, b):
@@ -18,7 +22,7 @@
 def main_kernel(
     bc_ref, order_ref, x_ref, out_ref,
     slots, a_buf, o_buf, acc_s, acc_x, rs, rx, tsum, sum_acc, s_mine, s_oth, s_tot, s_col,
-    st_send, st_recv, y_send, y_recv, c_send, c_recv, t_send, t_recv, s_send, s_recv,
+    st_send, st_recv, y_send, y_recv, c_send, c_recv, t_send, t_recv, z_recv, s_send, s_recv,
 ):
     nblk, panel, _ = slots.shape
     nsrc = nblk // 2
@@ -57,7 +61,11 @@
 
     blk_dev = x_ref.shape[1] // BLOCK
 
-    def fill(s, carry):
+    def target(i):
+        return (b + i * STRIDE) % nblk
+
+    def fill(i, carry):
+        s = target(i)
         cyc = order_ref[s]
         first = jnp.int32(-1)
         second = jnp.int32(-1)
@@ -72,34 +80,24 @@
             slots[s, :, pl.ds(r * BLOCK, BLOCK)] = block.astype(jnp.bfloat16)
         return carry
 
-    lax.fori_loop(0, nblk, fill, 0)
-
-    def clear(u, carry):
-        acc_s[u] = jnp.zeros((half, half), jnp.float32)
-        acc_x[u] = jnp.zeros((half, half), jnp.float32)
-        return carry
-
-    lax.fori_loop(0, NY, clear, 0)
-    sum_acc[...] = jnp.zeros(sum_acc.shape, jnp.float32)
+    lax.fori_loop(0, AHEAD, fill, 0)
 
     pl.semaphore_wait(barrier, (nblk - 1) * 4 + 3 + (NY - 1))
 
     my_rows = pl.ds(pl.multiple_of(c * panel, panel), panel)
     my_cols = pl.ds(pl.multiple_of(bm * W, W), W)
 
-    def st_copy(k, d):
-        s = (b + k) % nblk
+    def st_copy(i, d):
+        s = target(i)
         dst = a_buf.at[y, my_rows, my_cols] if d == 0 else o_buf.at[my_rows, my_cols]
         return pltpu.make_async_remote_copy(
             src_ref=slots.at[s],
             dst_ref=dst,
-            send_sem=st_send.at[d, k],
+            send_sem=st_send.at[d, i],
             recv_sem=st_recv.at[d, bm, c],
             device_id=(s, tm_of(y, h if d == 0 else 1 - h, bp)),
             device_id_type=MESH,
         )
-
-    st_copy(0, 1).start()
 
     @pl.when(bp == c)
     def _():
@@ -111,12 +109,29 @@
     def _():
         st_copy(0, 0).start()
 
-    def send_one(k, carry):
-        for d in range(2):
-            st_copy(k, d).start()
-        return carry
-
-    lax.fori_loop(1, nblk, send_one, 0)
+    def send_one(i, carry):
+        @pl.when(i + AHEAD - 1 < nblk)
+        def _():
+            fill(i + AHEAD - 1, 0)
+
+        @pl.when(i < nblk)
+        def _():
+            st_copy(i, 0).start()
+
+        @pl.when(i >= LAG)
+        def _():
+            st_copy(i - LAG, 1).start()
+        return carry
+
+    lax.fori_loop(1, nblk + LAG, send_one, 0)
+
+    def clear(u, carry):
+        acc_s[u] = jnp.zeros((half, half), jnp.float32)
+        acc_x[u] = jnp.zeros((half, half), jnp.float32)
+        return carry
+
+    lax.fori_loop(0, NY, clear, 0)
+    sum_acc[...] = jnp.zeros(sum_acc.shape, jnp.float32)
 
     def st_wait(d, m, q):
         rows = pl.ds(q * panel, panel)
@@ -143,10 +158,19 @@
         )
 
     def source(j):
-        k = 2 * j + (b + c) % 2
+        k = (2 * j + (b + c) % 2) * STRIDE % nblk
         return ((b + nblk - k) % nblk) // 2
 
     ones = jnp.ones((8, W), jnp.bfloat16)
+
+    first = pl.ds(0, half - BLOCK)
+    last = pl.ds(half - BLOCK, BLOCK)
+
+    def split(u, v):
+        return jnp.logical_and(u < CUT, v >= CUT)
+
+    def near(u, v):
+        return jnp.logical_and(u <= v, jnp.logical_or(u >= CUT, v < CUT))
 
     def multiply(m):
         cols = pl.ds(pl.multiple_of(m * W, W), W)
@@ -155,9 +179,17 @@
             panel_u = a_buf[u, :, cols]
             sum_acc[u] += dot_t(ones, panel_u)
 
-            @pl.when(u <= y)
+            @pl.when(near(u, y))
             def _():
                 acc_x[u] += dot_t(panel_u, o_buf[:, cols])
+
+            @pl.when(split(u, y))
+            def _():
+                acc_x[u, :, first] += dot_t(panel_u, o_buf[first, cols])
+
+            @pl.when(split(y, u))
+            def _():
+                acc_x[u, :, 0:BLOCK] += dot_t(o_buf[:, cols], a_buf[u, last, cols])
 
             @pl.when(u >= y)
             def _():
@@ -228,10 +260,26 @@
             device_id=(b, tm_of(u, h, c)), device_id_type=MESH,
         )
 
+    def t_split(yy, u):
+        start = yy * 2 * half + (1 - h) * half
+        cols = pl.ds(pl.multiple_of(start, BLOCK), half - BLOCK)
+        return pltpu.make_async_remote_copy(
+            src_ref=tsum.at[u, :, first], dst_ref=out_ref.at[:, cols],
+            send_sem=t_send.at[u], recv_sem=t_recv.at[yy],
+            device_id=(b, tm_of(u, h, c)), device_id_type=MESH,
+        )
+
+    def z_copy(v, hh):
+        start = v * 2 * half + hh * half + half - BLOCK
+        cols = pl.ds(pl.multiple_of(start, BLOCK), BLOCK)
+        return pltpu.make_async_remote_copy(
+            src_ref=tsum.at[v, :, 0:BLOCK], dst_ref=out_ref.at[:, cols],
+            send_sem=t_send.at[v], recv_sem=z_recv.at[v],
+            device_id=(b, tm_of(y, 1 - h, c)), device_id_type=MESH,
+        )
+
     def share_cross(u, carry):
-        @pl.when(u <= y)
-        def _():
-            c_copy(1, u).start()
+        c_copy(1, u).start()
         return carry
 
     def share_same(u, carry):
@@ -250,17 +298,30 @@
         s_col[u] = total.T
     count = s_tot[0, 1:2, 0:1] * BLOCK
 
-    def scaled(g, u_row, u_col):
+    def scaled(g, u_row, u_col, cols):
         si = s_col[u_row, mine, 0:1]
-        sj = s_tot[u_col, 0:1, :]
+        sj = s_tot[u_col, 0:1, cols]
         return g * count / (si * sj)
 
     def back(u, carry):
-        @pl.when(u < y)
-        def _():
-            c_copy(1, u).wait_recv()
-            tsum[u] = scaled(acc_x[u, mine, :] + rx[u], u, NY)
+        c_copy(1, u).wait_recv()
+
+        @pl.when(jnp.logical_and(u < y, near(u, y)))
+        def _():
+            tsum[u] = scaled(acc_x[u, mine, :] + rx[u], u, NY, whole)
             t_copy(y, u).start()
+
+        @pl.when(split(u, y))
+        def _():
+            tsum[u, :, first] = scaled(acc_x[u, mine, first] + rx[u, :, first], u, NY, first)
+            t_split(y, u).start()
+
+        @pl.when(split(y, u))
+        def _():
+            tsum[u, :, 0:BLOCK] = scaled(
+                acc_x[u, mine, 0:BLOCK] + rx[u, :, 0:BLOCK], NY, u, last
+            )
+            z_copy(u, h).start()
         return carry
 
     lax.fori_loop(0, NY, back, 0)
@@ -279,15 +340,14 @@
         @pl.when(u >= y)
         def _():
             c_copy(0, u).wait_recv()
-            g = scaled(acc_s[u, mine, :] + rs[u], y, u)
+            g = scaled(acc_s[u, mine, :] + rs[u], y, u, whole)
             first_tile = u * 4 + h * 2
             tiles = first_tile + jnp.where(tile >= panel, 1, 0)
             out_ref[:, same_cols] = jnp.where(tiles >= t, g, 0.0)
 
         @pl.when(u == y)
         def _():
-            c_copy(1, u).wait_recv()
-            g = scaled(acc_x[u, mine, :] + rx[u], y, NY)
+            g = scaled(acc_x[u, mine, :] + rx[u], y, NY, whole)
             first_tile = u * 4 + (1 - h) * 2
             tiles = first_tile + jnp.where(tile >= panel, 1, 0)
             out_ref[:, cross_cols] = jnp.where(tiles >= t, g, 0.0)
@@ -296,25 +356,30 @@
     lax.fori_loop(0, NY, place, 0)
 
     def arrive(u, carry):
-        @pl.when(u > y)
+        @pl.when(jnp.logical_and(u > y, near(y, u)))
         def _():
             t_copy(u, y).wait_recv()
+
+        @pl.when(split(y, u))
+        def _():
+            t_split(u, y).wait_recv()
+            z_copy(u, 1 - h).wait_recv()
         return carry
 
     lax.fori_loop(0, NY, arrive, 0)
-
-    st_copy(0, 1).wait_send()
 
     @pl.when(bp != c)
     def _():
         st_copy(0, 0).wait_send()
 
-    def drain_one(k, carry):
-        for d in range(2):
-            st_copy(k, d).wait_send()
-        return carry
-
-    lax.fori_loop(1, nblk, drain_one, 0)
+    def drain_one(i, carry):
+        @pl.when(i >= 1)
+        def _():
+            st_copy(i, 0).wait_send()
+        st_copy(i, 1).wait_send()
+        return carry
+
+    lax.fori_loop(0, nblk, drain_one, 0)
 
     def drain_y(m, carry):
         y_copy(m, 0, y, whole, up).wait_send()
@@ -326,17 +391,23 @@
     lax.fori_loop(0, nsrc, drain_y, 0)
 
     def drain_c(u, carry):
-        @pl.when(u <= y)
-        def _():
-            c_copy(1, u).wait_send()
+        c_copy(1, u).wait_send()
 
         @pl.when(u >= y)
         def _():
             c_copy(0, u).wait_send()
 
-        @pl.when(u < y)
+        @pl.when(jnp.logical_and(u < y, near(u, y)))
         def _():
             t_copy(y, u).wait_send()
+
+        @pl.when(split(u, y))
+        def _():
+            t_split(y, u).wait_send()
+
+        @pl.when(split(y, u))
+        def _():
+            z_copy(u, h).wait_send()
         return carry
 
     lax.fori_loop(0, NY, drain_c, 0)
@@ -374,11 +445,11 @@
             dma((2, nblk)), dma((2, nsrc, 2)),
             dma((nsrc, 4)), dma((nsrc, 4)),
             dma((2, NY)), dma((2, NY)),
-            dma((NY,)), dma((NY,)),
+            dma((NY,)), dma((NY,)), dma((NY,)),
             dma, dma,
         ],
         compiler_params=pltpu.CompilerParams(
-            collective_id=0, has_side_effects=True, vmem_limit_bytes=56 << 20
+            collective_id=0, has_side_effects=True, vmem_limit_bytes=32 << 20
         ),
         name="exchange",
     )(block_cycle, cycle_order, intensity)

time: 122 us -> 112 us (0.918); the launches traced: 120 us -> 112 us
  Pallas kernels: 117 us -> 108 us
    pallas_call x1, Pallas kernels: 117 us -> 108 us  [on_device(): pl.pallas_call(main_kernel, out_shape=jax.ShapeDtypeStruct((panel, frames...]
    unnamed x1 -> x7, local copies, waits for them, and re-layouts: 3.3 us -> 3.85 us
where the time goes in v3:
time: 112 us
  Pallas kernels  108 us (96%)
  local copies, waits for them, and re-layouts  3.85 us (3%)
    pallas_call x1, Pallas kernels, on_device(): pl.pallas_call(main_kernel, out_shape=jax.ShapeDtypeStruct((panel, frames...  108 us
    unnamed x7, local copies, waits for them, and re-layouts  3.85 us

profile of v3, /device:TPU:1, one launch (start us, length us, event | category | flops | bytes accessed | tf_op | source)
XLA Modules:
  0.0 111.8 jit_solution(5344446329147619147)
XLA Ops:
  0.0 0.0 copy-start
  0.0 1.1 %copy-done = bf16[192,2048]{1,0:T(8,128)(2,1)S(1)} copy-done((bf16[192,2048]{1,0:T(8,128)(2,1)S(1)}, bf16[192,2048]{1,0:T(8,128)(2,1)}, u32[]{:S(2)}) %copy-start) | copy-done | bytes 786456
  1.1 0.0 copy-start.1
  1.1 0.7 copy-done.1
  1.8 0.0 copy-start.2
  1.8 0.7 copy-done.2
  2.4 107.9 %exchange.1 = f32[192,3072]{1,0:T(8,128)S(1)} custom-call(s32[16]{0:T(128)S(1)} %copy-done.1, s32[16]{0:T(128)S(1)} %copy-done.2, bf16[192,2048]{1,0:T(8,128)(2,1)S(1)} %copy-done), custom_call_target="tpu_custom_call" | custom-call | tf_op jit(solution)/shard_map/exchange/pallas_call | solution.py:426
  110.4 1.4 %copy.5 = f32[1,192,3072]{2,1,0:T(8,128)} copy(f32[1,192,3072]{2,1,0:T(8,128)S(1)} %bitcast.1) | data formatting | bytes 4718592
Async XLA Ops:
  0.0 1.1 %copy-start = (bf16[192,2048]{1,0:T(8,128)(2,1)S(1)}, bf16[192,2048]{1,0:T(8,128)(2,1)}, u32[]{:S(2)}) copy-start(bf16[192,2048]{1,0:T(8,128)(2,1)} %x_ref.1) | copy-start | bytes 2359300
  1.1 0.7 copy-start.1
  1.8 0.7 copy-start.2

commit v4 on v3

--- a/solution.py
+++ b/solution.py
@@ -20,9 +20,9 @@
 
 
 def main_kernel(
-    bc_ref, order_ref, x_ref, out_ref,
-    slots, a_buf, o_buf, acc_s, acc_x, rs, rx, tsum, sum_acc, s_mine, s_oth, s_tot, s_col,
-    st_send, st_recv, y_send, y_recv, c_send, c_recv, t_send, t_recv, z_recv, s_send, s_recv,
+    bc_hbm, order_hbm, x_hbm, out_ref,
+    bc_ref, order_ref, x_ref, slots, a_buf, o_buf, acc_s, acc_x, rs, rx, tsum, sum_acc, s_mine, s_oth, s_tot, s_col,
+    st_send, st_recv, y_send, y_recv, c_send, c_recv, t_send, t_recv, z_recv, s_send, s_recv, in_sem,
 ):
     nblk, panel, _ = slots.shape
     nsrc = nblk // 2
@@ -43,6 +43,13 @@
 
     other = (b, tm_of(y, h, 1 - c))
 
+    inputs = [
+        pltpu.make_async_copy(src, dst, in_sem.at[i])
+        for i, (src, dst) in enumerate(((bc_hbm, bc_ref), (order_hbm, order_ref), (x_hbm, x_ref)))
+    ]
+    for copy in inputs:
+        copy.start()
+
     barrier = pltpu.get_barrier_semaphore()
 
     def greet(k, carry):
@@ -80,6 +87,8 @@
             slots[s, :, pl.ds(r * BLOCK, BLOCK)] = block.astype(jnp.bfloat16)
         return carry
 
+    for copy in inputs:
+        copy.wait()
     lax.fori_loop(0, AHEAD, fill, 0)
 
     pl.semaphore_wait(barrier, (nblk - 1) * 4 + 3 + (NY - 1))
@@ -143,10 +152,9 @@
         ).wait_recv()
 
     whole = pl.ds(0, half)
-    low = pl.ds(0, panel)
-    high = pl.ds(panel, panel)
-
-    def y_copy(m, way, src_y, rows, to_y):
+
+    def y_copy(m, way, src_y, q, to_y):
+        rows = pl.ds(q * panel, panel)
         cols = pl.ds(pl.multiple_of(m * W, W), W)
         return pltpu.make_async_remote_copy(
             src_ref=a_buf.at[src_y, rows, cols],
@@ -172,61 +180,79 @@
     def near(u, v):
         return jnp.logical_and(u <= v, jnp.logical_or(u >= CUT, v < CUT))
 
-    def multiply(m):
+    def job(m, u):
         cols = pl.ds(pl.multiple_of(m * W, W), W)
-
-        def job(u, carry):
-            panel_u = a_buf[u, :, cols]
-            sum_acc[u] += dot_t(ones, panel_u)
-
-            @pl.when(near(u, y))
-            def _():
-                acc_x[u] += dot_t(panel_u, o_buf[:, cols])
-
-            @pl.when(split(u, y))
-            def _():
-                acc_x[u, :, first] += dot_t(panel_u, o_buf[first, cols])
-
-            @pl.when(split(y, u))
-            def _():
-                acc_x[u, :, 0:BLOCK] += dot_t(o_buf[:, cols], a_buf[u, last, cols])
-
-            @pl.when(u >= y)
-            def _():
-                acc_s[u] += dot_t(a_buf[y, :, cols], panel_u)
+        panel_u = a_buf[u, :, cols]
+        sum_acc[u] += dot_t(ones, panel_u)
+
+        @pl.when(near(u, y))
+        def _():
+            acc_x[u] += dot_t(panel_u, o_buf[:, cols])
+
+        @pl.when(split(u, y))
+        def _():
+            acc_x[u, :, first] += dot_t(panel_u, o_buf[first, cols])
+
+        @pl.when(split(y, u))
+        def _():
+            acc_x[u, :, 0:BLOCK] += dot_t(o_buf[:, cols], a_buf[u, last, cols])
+
+        @pl.when(u >= y)
+        def _():
+            acc_s[u] += dot_t(a_buf[y, :, cols], panel_u)
+
+    def neighbour(r):
+        return (y + r + r // 2) % NY
+
+    def multiply_near(m):
+        cols = pl.ds(pl.multiple_of(m * W, W), W)
+        sum_acc[NY] += dot_t(ones, o_buf[:, cols])
+
+        def one(r, carry):
+            job(m, neighbour(r))
             return carry
 
-        lax.fori_loop(0, NY, job, 0)
-        sum_acc[NY] += dot_t(ones, o_buf[:, cols])
+        lax.fori_loop(0, 3, one, 0)
+
+    def multiply_far(m):
+        y_copy(m, 4, far, 0, y).wait_recv()
+        y_copy(m, 5, far, 1, y).wait_recv()
+        job(m, far)
 
     def step(j, carry):
         @pl.when(j < nsrc)
         def _():
             m = source(j)
-            for q in range(2):
-                st_wait(0, m, q)
-            y_copy(m, 0, y, whole, up).start()
-            y_copy(m, 1, y, whole, down).start()
-
-        @pl.when(jnp.logical_and(j >= 1, j < nsrc + 1))
+            st_wait(0, m, 0)
+            y_copy(m, 0, y, 0, up).start()
+            st_wait(0, m, 1)
+            y_copy(m, 3, y, 1, down).start()
+            y_copy(m, 1, y, 1, up).start()
+            y_copy(m, 2, y, 0, down).start()
+
+        @pl.when(j >= 1)
         def _():
             m = source(j - 1)
-            y_copy(m, 0, down, whole, y).wait_recv()
-            y_copy(m, 2, down, low, up).start()
-            y_copy(m, 1, up, whole, y).wait_recv()
-            y_copy(m, 3, up, high, down).start()
+            y_copy(m, 0, down, 0, y).wait_recv()
+            y_copy(m, 4, down, 0, up).start()
+            y_copy(m, 3, up, 1, y).wait_recv()
+            y_copy(m, 5, up, 1, down).start()
 
         @pl.when(j >= 2)
         def _():
-            m = source(j - 2)
+            multiply_far(source(j - 2))
+
+        @pl.when(j >= 1)
+        def _():
+            m = source(j - 1)
+            y_copy(m, 1, down, 1, y).wait_recv()
+            y_copy(m, 2, up, 0, y).wait_recv()
             for q in range(2):
                 st_wait(1, m, q)
-            y_copy(m, 2, far, low, y).wait_recv()
-            y_copy(m, 3, far, high, y).wait_recv()
-            multiply(m)
-        return carry
-
-    lax.fori_loop(0, nsrc + 2, step, 0)
+            multiply_near(m)
+        return carry
+
+    lax.fori_loop(0, nsrc + 1, step, 0)
 
     theirs = pl.ds(pl.multiple_of((1 - c) * panel, panel), panel)
     mine = pl.ds(pl.multiple_of(c * panel, panel), panel)
@@ -236,13 +262,23 @@
     row = lax.broadcasted_iota(jnp.int32, head.shape, 0)
     mark = jnp.where(jnp.logical_and(lane % BLOCK == 0, row == 0), head, 0.0)
     filled = jnp.sum(jnp.where(mark > 0.0, 1.0, 0.0))
-    srow = lax.broadcasted_iota(jnp.int32, sum_acc.shape, 1)
-    s_mine[...] = jnp.where(srow == 1, filled, sum_acc[...])
-    s_copy = pltpu.make_async_remote_copy(
-        src_ref=s_mine, dst_ref=s_oth, send_sem=s_send, recv_sem=s_recv,
-        device_id=other, device_id_type=MESH,
-    )
-    s_copy.start()
+    srow = lax.broadcasted_iota(jnp.int32, (8, half), 0)
+
+    def s_copy(u):
+        return pltpu.make_async_remote_copy(
+            src_ref=s_mine.at[u], dst_ref=s_oth.at[u], send_sem=s_send.at[u], recv_sem=s_recv.at[u],
+            device_id=other, device_id_type=MESH,
+        )
+
+    def share_sum(u):
+        s_mine[u] = jnp.where(srow == 1, filled, sum_acc[u])
+        s_copy(u).start()
+
+    def take_sum(u):
+        s_copy(u).wait_recv()
+        total = s_mine[u] + s_oth[u]
+        s_tot[u] = total
+        s_col[u] = total.T
 
     def c_copy(kind, u):
         src, dst = (acc_s, rs) if kind == 0 else (acc_x, rx)
@@ -278,32 +314,19 @@
             device_id=(b, tm_of(y, 1 - h, c)), device_id_type=MESH,
         )
 
-    def share_cross(u, carry):
+    def share(u):
         c_copy(1, u).start()
-        return carry
-
-    def share_same(u, carry):
+
         @pl.when(u >= y)
         def _():
             c_copy(0, u).start()
-        return carry
-
-    lax.fori_loop(0, NY, share_cross, 0)
-    lax.fori_loop(0, NY, share_same, 0)
-
-    s_copy.wait_recv()
-    for u in range(NY + 1):
-        total = s_mine[u] + s_oth[u]
-        s_tot[u] = total
-        s_col[u] = total.T
-    count = s_tot[0, 1:2, 0:1] * BLOCK
 
     def scaled(g, u_row, u_col, cols):
         si = s_col[u_row, mine, 0:1]
         sj = s_tot[u_col, 0:1, cols]
-        return g * count / (si * sj)
-
-    def back(u, carry):
+        return g * (s_tot[NY, 1:2, 0:1] * BLOCK) / (si * sj)
+
+    def back(u):
         c_copy(1, u).wait_recv()
 
         @pl.when(jnp.logical_and(u < y, near(u, y)))
@@ -322,9 +345,35 @@
                 acc_x[u, mine, 0:BLOCK] + rx[u, :, 0:BLOCK], NY, u, last
             )
             z_copy(u, h).start()
-        return carry
-
-    lax.fori_loop(0, NY, back, 0)
+
+    share_sum(NY)
+
+    def share_near(r, carry):
+        share_sum(neighbour(r))
+        return carry
+
+    def share_blocks(r, carry):
+        share(neighbour(r))
+        return carry
+
+    def take_near(r, carry):
+        take_sum(neighbour(r))
+        return carry
+
+    def back_near(r, carry):
+        back(neighbour(r))
+        return carry
+
+    lax.fori_loop(0, 3, share_near, 0)
+    lax.fori_loop(0, 3, share_blocks, 0)
+    take_sum(NY)
+    lax.fori_loop(0, 3, take_near, 0)
+    lax.fori_loop(0, 3, back_near, 0)
+    multiply_far(source(nsrc - 1))
+    share_sum(far)
+    share(far)
+    take_sum(far)
+    back(far)
 
     tile = lax.broadcasted_iota(jnp.int32, (panel, half), 1)
 
@@ -382,10 +431,12 @@
     lax.fori_loop(0, nblk, drain_one, 0)
 
     def drain_y(m, carry):
-        y_copy(m, 0, y, whole, up).wait_send()
-        y_copy(m, 1, y, whole, down).wait_send()
-        y_copy(m, 2, down, low, up).wait_send()
-        y_copy(m, 3, up, high, down).wait_send()
+        y_copy(m, 0, y, 0, up).wait_send()
+        y_copy(m, 1, y, 1, up).wait_send()
+        y_copy(m, 2, y, 0, down).wait_send()
+        y_copy(m, 3, y, 1, down).wait_send()
+        y_copy(m, 4, down, 0, up).wait_send()
+        y_copy(m, 5, up, 1, down).wait_send()
         return carry
 
     lax.fori_loop(0, nsrc, drain_y, 0)
@@ -411,7 +462,8 @@
         return carry
 
     lax.fori_loop(0, NY, drain_c, 0)
-    s_copy.wait_send()
+    for u in range(NY + 1):
+        s_copy(u).wait_send()
 
 
 def on_device(intensity, block_cycle, cycle_order):
@@ -421,14 +473,17 @@
     half = 2 * panel
     frames = panel * lax.axis_size("tm")
     vmem = pl.BlockSpec(memory_space=pltpu.VMEM)
-    smem = pl.BlockSpec(memory_space=pltpu.SMEM)
+    hbm = pl.BlockSpec(memory_space=pltpu.HBM)
     dma = pltpu.SemaphoreType.DMA
     twotime = pl.pallas_call(
         main_kernel,
         out_shape=jax.ShapeDtypeStruct((panel, frames), jnp.float32),
-        in_specs=[smem, smem, vmem],
+        in_specs=[hbm, hbm, hbm],
         out_specs=vmem,
         scratch_shapes=[
+            pltpu.SMEM(block_cycle.shape, jnp.int32),
+            pltpu.SMEM(cycle_order.shape, jnp.int32),
+            pltpu.VMEM(intensity.shape, jnp.bfloat16),
             pltpu.VMEM((nblk, panel, W), jnp.bfloat16),
             pltpu.VMEM((NY, half, nsrc * W), jnp.bfloat16),
             pltpu.VMEM((half, nsrc * W), jnp.bfloat16),
@@ -443,16 +498,16 @@
             pltpu.VMEM((NY + 1, 8, half), jnp.float32),
             pltpu.VMEM((NY + 1, half, 8), jnp.float32),
             dma((2, nblk)), dma((2, nsrc, 2)),
-            dma((nsrc, 4)), dma((nsrc, 4)),
+            dma((nsrc, 6)), dma((nsrc, 6)),
             dma((2, NY)), dma((2, NY)),
             dma((NY,)), dma((NY,)), dma((NY,)),
-            dma, dma,
+            dma((NY + 1,)), dma((NY + 1,)), dma((3,)),
         ],
         compiler_params=pltpu.CompilerParams(
             collective_id=0, has_side_effects=True, vmem_limit_bytes=32 << 20
         ),
         name="exchange",
-    )(block_cycle, cycle_order, intensity)
+    )(*(pltpu.with_memory_space_constraint(a, pltpu.HBM) for a in (block_cycle, cycle_order, intensity)))
     return twotime.reshape(1, panel, frames)
 
 

time: 112 us -> 108 us (0.964); the launches traced: 112 us -> 106 us
  Pallas kernels: 108 us -> 105 us
  local copies, waits for them, and re-layouts: 3.85 us -> 1.41 us
    pallas_call x1, Pallas kernels: 108 us -> 105 us  [on_device(): pl.pallas_call(main_kernel, out_shape=jax.ShapeDtypeStruct((panel, frames...]
    unnamed x7 -> x1, local copies, waits for them, and re-layouts: 3.85 us -> 1.41 us
where the time goes in v4:
time: 108 us; the launch traced here: 106 us
  Pallas kernels  105 us (97%)
  local copies, waits for them, and re-layouts  1.41 us (1%)
    pallas_call x1, Pallas kernels, on_device(): pl.pallas_call(main_kernel, out_shape=jax.ShapeDtypeStruct((panel, frames...  105 us

profile of v4, /device:TPU:1, one launch (start us, length us, event | category | flops | bytes accessed | tf_op | source)
XLA Modules:
  0.0 106.0 jit_solution(11987452135705736070)
XLA Ops:
  0.0 104.6 %exchange.1 = f32[192,3072]{1,0:T(8,128)S(1)} custom-call(s32[16]{0:T(128)} %bc_hbm.1, s32[16]{0:T(128)} %order_hbm.1, bf16[192,2048]{1,0:T(8,128)(2,1)} %x_hbm.1), custom_call_target="tpu_custom_call" | custom-call | tf_op jit(solution)/shard_map/exchange/pallas_call | solution.py:478
  104.6 1.4 %copy.5 = f32[1,192,3072]{2,1,0:T(8,128)} copy(f32[1,192,3072]{2,1,0:T(8,128)S(1)} %bitcast.1) | data formatting | bytes 4718592

commit v5 on v4

--- a/solution.py
+++ b/solution.py
@@ -180,33 +180,52 @@
     def near(u, v):
         return jnp.logical_and(u <= v, jnp.logical_or(u >= CUT, v < CUT))
 
+    def job_sum(m, u):
+        cols = pl.ds(pl.multiple_of(m * W, W), W)
+        sum_acc[u] += dot_t(ones, a_buf[u, :, cols])
+
+    def job_cross(m, u):
+        cols = pl.ds(pl.multiple_of(m * W, W), W)
+
+        @pl.when(near(u, y))
+        def _():
+            acc_x[u] += dot_t(a_buf[u, :, cols], o_buf[:, cols])
+
+        @pl.when(split(u, y))
+        def _():
+            acc_x[u, :, first] += dot_t(a_buf[u, :, cols], o_buf[first, cols])
+
+        @pl.when(split(y, u))
+        def _():
+            acc_x[u, :, 0:BLOCK] += dot_t(o_buf[:, cols], a_buf[u, last, cols])
+
+    def job_same(m, u):
+        cols = pl.ds(pl.multiple_of(m * W, W), W)
+
+        @pl.when(u >= y)
+        def _():
+            acc_s[u] += dot_t(a_buf[y, :, cols], a_buf[u, :, cols])
+
     def job(m, u):
-        cols = pl.ds(pl.multiple_of(m * W, W), W)
-        panel_u = a_buf[u, :, cols]
-        sum_acc[u] += dot_t(ones, panel_u)
-
-        @pl.when(near(u, y))
-        def _():
-            acc_x[u] += dot_t(panel_u, o_buf[:, cols])
-
-        @pl.when(split(u, y))
-        def _():
-            acc_x[u, :, first] += dot_t(panel_u, o_buf[first, cols])
-
-        @pl.when(split(y, u))
-        def _():
-            acc_x[u, :, 0:BLOCK] += dot_t(o_buf[:, cols], a_buf[u, last, cols])
-
-        @pl.when(u >= y)
-        def _():
-            acc_s[u] += dot_t(a_buf[y, :, cols], panel_u)
+        job_sum(m, u)
+        job_cross(m, u)
+        job_same(m, u)
 
     def neighbour(r):
         return (y + r + r // 2) % NY
 
-    def multiply_near(m):
+    def other_sum(m):
         cols = pl.ds(pl.multiple_of(m * W, W), W)
         sum_acc[NY] += dot_t(ones, o_buf[:, cols])
+
+    def await_near(m):
+        y_copy(m, 1, down, 1, y).wait_recv()
+        y_copy(m, 2, up, 0, y).wait_recv()
+        for q in range(2):
+            st_wait(1, m, q)
+
+    def multiply_near(m):
+        other_sum(m)
 
         def one(r, carry):
             job(m, neighbour(r))
@@ -242,13 +261,10 @@
         def _():
             multiply_far(source(j - 2))
 
-        @pl.when(j >= 1)
+        @pl.when(jnp.logical_and(j >= 1, j < nsrc))
         def _():
             m = source(j - 1)
-            y_copy(m, 1, down, 1, y).wait_recv()
-            y_copy(m, 2, up, 0, y).wait_recv()
-            for q in range(2):
-                st_wait(1, m, q)
+            await_near(m)
             multiply_near(m)
         return carry
 
@@ -257,6 +273,7 @@
     theirs = pl.ds(pl.multiple_of((1 - c) * panel, panel), panel)
     mine = pl.ds(pl.multiple_of(c * panel, panel), panel)
 
+    end = source(nsrc - 1)
     head = a_buf[y, 0:16, :].astype(jnp.float32)
     lane = lax.broadcasted_iota(jnp.int32, head.shape, 1)
     row = lax.broadcasted_iota(jnp.int32, head.shape, 0)
@@ -314,9 +331,7 @@
             device_id=(b, tm_of(y, 1 - h, c)), device_id_type=MESH,
         )
 
-    def share(u):
-        c_copy(1, u).start()
-
+    def share_same(u):
         @pl.when(u >= y)
         def _():
             c_copy(0, u).start()
@@ -346,32 +361,47 @@
             )
             z_copy(u, h).start()
 
+    await_near(end)
+    other_sum(end)
     share_sum(NY)
 
-    def share_near(r, carry):
+    def near_sum(r, carry):
+        job_sum(end, neighbour(r))
         share_sum(neighbour(r))
         return carry
 
-    def share_blocks(r, carry):
-        share(neighbour(r))
-        return carry
-
-    def take_near(r, carry):
+    def near_cross(r, carry):
+        job_cross(end, neighbour(r))
+        c_copy(1, neighbour(r)).start()
+        return carry
+
+    def near_same(r, carry):
+        job_same(end, neighbour(r))
+        share_same(neighbour(r))
+        return carry
+
+    def near_take(r, carry):
         take_sum(neighbour(r))
         return carry
 
-    def back_near(r, carry):
+    def near_back(r, carry):
         back(neighbour(r))
         return carry
 
-    lax.fori_loop(0, 3, share_near, 0)
-    lax.fori_loop(0, 3, share_blocks, 0)
+    lax.fori_loop(0, 3, near_sum, 0)
+    lax.fori_loop(0, 3, near_cross, 0)
+    lax.fori_loop(0, 3, near_same, 0)
     take_sum(NY)
-    lax.fori_loop(0, 3, take_near, 0)
-    lax.fori_loop(0, 3, back_near, 0)
-    multiply_far(source(nsrc - 1))
+    lax.fori_loop(0, 3, near_take, 0)
+    lax.fori_loop(0, 3, near_back, 0)
+    y_copy(end, 4, far, 0, y).wait_recv()
+    y_copy(end, 5, far, 1, y).wait_recv()
+    job_sum(end, far)
     share_sum(far)
-    share(far)
+    job_cross(end, far)
+    c_copy(1, far).start()
+    job_same(end, far)
+    share_same(far)
     take_sum(far)
     back(far)
 
@@ -403,19 +433,6 @@
         return carry
 
     lax.fori_loop(0, NY, place, 0)
-
-    def arrive(u, carry):
-        @pl.when(jnp.logical_and(u > y, near(y, u)))
-        def _():
-            t_copy(u, y).wait_recv()
-
-        @pl.when(split(y, u))
-        def _():
-            t_split(u, y).wait_recv()
-            z_copy(u, 1 - h).wait_recv()
-        return carry
-
-    lax.fori_loop(0, NY, arrive, 0)
 
     @pl.when(bp != c)
     def _():
@@ -440,6 +457,19 @@
         return carry
 
     lax.fori_loop(0, nsrc, drain_y, 0)
+
+    def arrive(u, carry):
+        @pl.when(jnp.logical_and(u > y, near(y, u)))
+        def _():
+            t_copy(u, y).wait_recv()
+
+        @pl.when(split(y, u))
+        def _():
+            t_split(u, y).wait_recv()
+            z_copy(u, 1 - h).wait_recv()
+        return carry
+
+    lax.fori_loop(0, NY, arrive, 0)
 
     def drain_c(u, carry):
         c_copy(1, u).wait_send()

time: 108 us -> 107 us (level)
  no operation moved by 1% of the time
where the time goes in v5:
time: 107 us; the launch traced here: 106 us
  Pallas kernels  104 us (97%)
  local copies, waits for them, and re-layouts  1.41 us (1%)
    pallas_call x1, Pallas kernels, on_device(): pl.pallas_call(main_kernel, out_shape=jax.ShapeDtypeStruct((panel, frames...  104 us

profile of v5, /device:TPU:1, one launch (start us, length us, event | category | flops | bytes accessed | tf_op | source)
XLA Modules:
  0.0 105.6 jit_solution(14501836583490213591)
XLA Ops:
  0.0 104.1 %exchange.1 = f32[192,3072]{1,0:T(8,128)S(1)} custom-call(s32[16]{0:T(128)} %bc_hbm.1, s32[16]{0:T(128)} %order_hbm.1, bf16[192,2048]{1,0:T(8,128)(2,1)} %x_hbm.1), custom_call_target="tpu_custom_call" | custom-call | tf_op jit(solution)/shard_map/exchange/pallas_call | solution.py:508
  104.1 1.4 %copy.5 = f32[1,192,3072]{2,1,0:T(8,128)} copy(f32[1,192,3072]{2,1,0:T(8,128)S(1)} %bitcast.1) | data formatting | bytes 4718592

commit v6 on v5

--- a/solution.py
+++ b/solution.py
@@ -53,14 +53,25 @@
     barrier = pltpu.get_barrier_semaphore()
 
     def greet(k, carry):
-        s = (b + k) % nblk
+        s = (bm + k) % nsrc * 2 + c
         for j in range(4):
             pl.semaphore_signal(barrier, inc=1, device_id=(s, y * 4 + j), device_id_type=MESH)
         return carry
 
-    lax.fori_loop(1, nblk, greet, 0)
-    for j in range(1, 4):
-        pl.semaphore_signal(barrier, inc=1, device_id=(b, y * 4 + (t + j) % 4), device_id_type=MESH)
+    @pl.when(bp == c)
+    def _():
+        for j in range(1, 4):
+            to = (b, y * 4 + (t + j) % 4)
+            pl.semaphore_signal(barrier, inc=1, device_id=to, device_id_type=MESH)
+
+    @pl.when(bp != c)
+    def _():
+        greet(0, 0)
+        pl.semaphore_signal(barrier, inc=1, device_id=other, device_id_type=MESH)
+        to = (b, tm_of(y, 1 - h, c))
+        pl.semaphore_signal(barrier, inc=1, device_id=to, device_id_type=MESH)
+
+    lax.fori_loop(1, nsrc, greet, 0)
     for r in range(1, NY):
         pl.semaphore_signal(
             barrier, inc=1, device_id=(b, tm_of((y + r) % NY, h, c)), device_id_type=MESH
@@ -91,7 +102,7 @@
         copy.wait()
     lax.fori_loop(0, AHEAD, fill, 0)
 
-    pl.semaphore_wait(barrier, (nblk - 1) * 4 + 3 + (NY - 1))
+    pl.semaphore_wait(barrier, nblk * 2 + NY - 1 + jnp.where(bp == c, 0, 1))
 
     my_rows = pl.ds(pl.multiple_of(c * panel, panel), panel)
     my_cols = pl.ds(pl.multiple_of(bm * W, W), W)

time: 107 us -> 106 us (level)
  no operation moved by 1% of the time
where the time goes in v6:
time: 106 us; the launch traced here: 105 us
  Pallas kernels  104 us (98%)
  local copies, waits for them, and re-layouts  1.41 us (1%)
    pallas_call x1, Pallas kernels, on_device(): pl.pallas_call(main_kernel, out_shape=jax.ShapeDtypeStruct((panel, frames...  104 us

profile of v6, /device:TPU:1, one launch (start us, length us, event | category | flops | bytes accessed | tf_op | source)
XLA Modules:
  0.0 105.1 jit_solution(11876682506612128410)
XLA Ops:
  0.0 103.7 %exchange.1 = f32[192,3072]{1,0:T(8,128)S(1)} custom-call(s32[16]{0:T(128)} %bc_hbm.1, s32[16]{0:T(128)} %order_hbm.1, bf16[192,2048]{1,0:T(8,128)(2,1)} %x_hbm.1), custom_call_target="tpu_custom_call" | custom-call | tf_op jit(solution)/shard_map/exchange/pallas_call | solution.py:519
  103.7 1.4 %copy.5 = f32[1,192,3072]{2,1,0:T(8,128)} copy(f32[1,192,3072]{2,1,0:T(8,128)S(1)} %bitcast.1) | data formatting | bytes 4718592

commit v7 on v6

--- a/solution.py
+++ b/solution.py
@@ -223,7 +223,7 @@
         job_same(m, u)
 
     def neighbour(r):
-        return (y + r + r // 2) % NY
+        return (y + 1 + r + (r + 1) // 2) % NY
 
     def other_sum(m):
         cols = pl.ds(pl.multiple_of(m * W, W), W)

time: 106 us -> 106 us (level)
  no operation moved by 1% of the time
where the time goes in v7:
time: 106 us; the launch traced here: 104 us
  Pallas kernels  103 us (97%)
  local copies, waits for them, and re-layouts  1.41 us (1%)
    pallas_call x1, Pallas kernels, on_device(): pl.pallas_call(main_kernel, out_shape=jax.ShapeDtypeStruct((panel, frames...  103 us

profile of v7, /device:TPU:1, one launch (start us, length us, event | category | flops | bytes accessed | tf_op | source)
XLA Modules:
  0.0 104.2 jit_solution(8054024410381237349)
XLA Ops:
  0.0 102.8 %exchange.1 = f32[192,3072]{1,0:T(8,128)S(1)} custom-call(s32[16]{0:T(128)} %bc_hbm.1, s32[16]{0:T(128)} %order_hbm.1, bf16[192,2048]{1,0:T(8,128)(2,1)} %x_hbm.1), custom_call_target="tpu_custom_call" | custom-call | tf_op jit(solution)/shard_map/exchange/pallas_call | solution.py:519
  102.8 1.4 %copy.5 = f32[1,192,3072]{2,1,0:T(8,128)} copy(f32[1,192,3072]{2,1,0:T(8,128)S(1)} %bitcast.1) | data formatting | bytes 4718592
